TPU v7x, 512 devices: a whole 4x8x8 slice. The times are simulated.
512 devices in a mesh: rel: 16 (over z, core), dev: 32 (over y, x).
Axes of the slice: x: 4, y: 8, z: 8, core: 2. Of those that a mesh axis runs over, the one named last changes fastest.
Arguments:
- src_feat: bfloat16 [16, 8192, 1024], P('rel', 'dev'), may hold values from -6 to 6
- rel_w_in: bfloat16 [16, 1024, 1024], P('rel', 'dev'), may hold values from -0.1875 to 0.1875
- rel_w_out: bfloat16 [16, 1024, 1024], P('rel', 'dev'), may hold values from -0.1875 to 0.1875
- tile_source: int32 [16, 128], P('rel'), may hold values from 0 to 63
- tile_edges: int32 [16, 128, 128], P('rel'), may hold values from 0 to 16383
- tile_count: int32 [16, 128], P('rel'), may hold values from 0 to 128, as said below
- target_feat: bfloat16 [4096, 1024], P(('dev', 'rel')), may hold values from -6 to 6
- norm_gain: float32 [1024], replicated, may hold values from 0.5 to 2
- tgt_w_in: bfloat16 [1024, 2048], P(None, 'rel'), may hold values from -0.1875 to 0.1875
- tgt_w_out: bfloat16 [2048, 1024], P('rel'), may hold values from -0.125 to 0.125
- out_grad: bfloat16 [4096, 1024], P(('dev', 'rel')), may hold values from -6 to 6
Outputs:
- updated: bfloat16 [4096, 1024], P(('dev', 'rel'))
- src_grad: bfloat16 [16, 8192, 1024], P('rel', 'dev')
Inputs may be any that keep to these rules, and one draw needn't show every extreme that they name: Tile k of a relation joins target rows 128 * (k // 4) onward with source rows 128 * tile_source onward. `tile_edges`: each entry is t * 128 + s for an edge from in-tile source offset s to in-tile target offset t; entries past a tile's count are ignored; the same edge may stand several times. The first tile_count entries of a tile's row of tile_edges are its edges; 0 marks an empty tile; in every relation some tile holds 128 edges.
All inputs are finite; a program needn't handle non-finite values.
Results may differ from a plain program's by a relative error of at most 0.013.
Values may be sent and summed in bfloat16 or wider, within the bound.
A program may use at most 64 MiB of HBM per device.

v0:
```python
import jax
import jax.numpy as jnp
from jax import lax
from jax.sharding import PartitionSpec as P

TILE = 128
TILE_ROW = 4


eps_norm = 1e-06


def in_one_piece(arrays, axis, dim, along):
    both = jnp.concatenate(arrays, axis=along)
    whole, at, gathered = (lax.all_gather(both, axis, axis=dim, tiled=True), 0, [])
    for a in arrays:
        gathered.append(lax.slice_in_dim(whole, at, at + a.shape[along], axis=along))
        at += a.shape[along]
    return tuple(gathered)


def cut_along(array, dim, length):
    dims = array.shape
    parts = array.reshape(*dims[:dim], length, dims[dim] // length, *dims[dim + 1 :])
    return jnp.moveaxis(parts, dim, 0)


def sent_and_summed(array, axis, dim):
    parts = cut_along(array, dim, lax.axis_size(axis))
    arrived = lax.all_to_all(parts, axis, split_axis=0, concat_axis=0, tiled=True)
    return arrived.sum(axis=0)


def laid_out(parts, dim):
    dims = list(parts.shape[1:])
    dims[dim] *= parts.shape[0]
    return jnp.moveaxis(parts, 0, dim).reshape(dims)


def from_everyone(array, axis):
    length = lax.axis_size(axis)
    return lax.all_to_all(
        jnp.broadcast_to(array[None], (length, *array.shape)), axis, 0, 0, tiled=True
    )


def collect(array, axis, dim):
    return laid_out(from_everyone(array, axis), dim)


def summed_on_arrival(array, axis, dim):
    parts = cut_along(array, dim, lax.axis_size(axis))
    arrived = lax.all_to_all(parts, axis, split_axis=0, concat_axis=0, tiled=True)
    return arrived.astype(jnp.float32).sum(axis=0)


def silu_slope(values):
    sigma = jax.nn.sigmoid(values)
    return sigma * (1.0 + values * (1.0 - sigma))


def tile_counts(edge_codes, live_counts):
    live_mask = lax.broadcasted_iota(jnp.int32, edge_codes.shape, 1) < live_counts[:, None]
    lattice = lax.broadcasted_iota(jnp.int32, (1, 1, TILE), 2)
    target_hot = (((edge_codes // TILE)[:, :, None] == lattice) & live_mask[:, :, None]).astype(
        jnp.bfloat16
    )
    source_hot = ((edge_codes % TILE)[:, :, None] == lattice).astype(jnp.bfloat16)
    counts = jnp.einsum("kes,ket->kst", source_hot, target_hot, preferred_element_type=jnp.float32)
    return counts.astype(jnp.bfloat16)


def aggregate(features, source_ids, all_counts):
    breadth = features.shape[0]
    source_total = features.shape[1]
    block_count = source_ids.shape[0] // TILE_ROW
    per_turn = 8 * TILE_ROW
    source_blocks = features.reshape(breadth, source_total // TILE, TILE)

    def aggregate_advance(iteration, running):
        offset = iteration * per_turn
        chosen = lax.dynamic_slice_in_dim(source_ids, offset, per_turn, 0)
        counts = lax.dynamic_slice_in_dim(all_counts, offset, per_turn, 0).reshape(
            8, TILE_ROW, TILE, TILE
        )
        picked = jnp.take(source_blocks, chosen, axis=1).reshape(breadth, 8, TILE_ROW, TILE)
        contrib = jnp.einsum("fbjs,bjst->fbt", picked, counts, preferred_element_type=jnp.float32)
        return lax.dynamic_update_slice_in_dim(
            running, contrib.reshape(breadth, 8 * TILE), iteration * 8 * TILE, 1
        )

    running = jnp.zeros((breadth, block_count * TILE), jnp.float32)
    return lax.fori_loop(0, block_count // 8, aggregate_advance, running)


def spread(grad_targets, source_ids, all_counts, source_total):
    breadth = grad_targets.shape[0]
    block_count = source_ids.shape[0] // TILE_ROW
    per_turn = 8 * TILE_ROW
    source_blocks = source_total // TILE
    target_blocks = grad_targets.reshape(breadth, block_count, TILE)

    def spread_advance(iteration, running):
        offset = iteration * per_turn
        chosen = lax.dynamic_slice_in_dim(source_ids, offset, per_turn, 0)
        counts = lax.dynamic_slice_in_dim(all_counts, offset, per_turn, 0).reshape(
            8, TILE_ROW, TILE, TILE
        )
        target_part = lax.dynamic_slice_in_dim(target_blocks, iteration * 8, 8, 1)
        pieces = jnp.einsum(
            "fbt,bjst->fbjs", target_part, counts, preferred_element_type=jnp.float32
        )
        pieces = pieces.reshape(breadth, per_turn, TILE)
        return running.at[:, chosen, :].add(pieces)

    running = jnp.zeros((breadth, source_blocks, TILE), jnp.float32)
    return lax.fori_loop(0, block_count // 8, spread_advance, running).reshape(
        breadth, source_total
    )


def shards(
    src_feat,
    rel_w_in,
    rel_w_out,
    tile_source,
    tile_edges,
    tile_count,
    target_feat,
    norm_gain,
    tgt_w_in,
    tgt_w_out,
    out_grad,
):
    own_rows = src_feat[0]
    in_slice = rel_w_in[0]
    out_slice = rel_w_out[0]
    source_ids = tile_source[0]
    edge_codes = tile_edges[0]
    live_counts = tile_count[0]
    model_width = own_rows.shape[1]
    device_count = lax.axis_size("dev")
    relation_count = lax.axis_size("rel")
    in_full, out_full = in_one_piece((in_slice, out_slice), "dev", 0, 1)
    hidden_pre = jnp.dot(own_rows, in_full, preferred_element_type=jnp.float32)
    hidden = jax.nn.silu(hidden_pre).astype(jnp.bfloat16)
    mixed_cols = lax.dot_general(
        out_full, hidden, (((0,), (1,)), ((), ())), preferred_element_type=jnp.float32
    )
    mixed_cols = mixed_cols.astype(jnp.bfloat16)
    all_counts = tile_counts(edge_codes, live_counts)
    by_feature = lax.all_to_all(mixed_cols, "dev", split_axis=0, concat_axis=1, tiled=True)
    partial_value = aggregate(by_feature, source_ids, all_counts)
    feature_width = partial_value.shape[0]
    source_total = by_feature.shape[1]
    target_total = partial_value.shape[1]
    target_rows = target_total // device_count
    share_rows = target_rows // relation_count
    gain_column = norm_gain[:, None]
    split_view = partial_value.reshape(feature_width, device_count, relation_count, share_rows)
    shared_sum = sent_and_summed(split_view, "rel", 2)
    agg_cols = lax.all_to_all(shared_sum, "dev", split_axis=1, concat_axis=0, tiled=True).reshape(
        model_width, share_rows
    )
    inverse_norm = lax.rsqrt(jnp.mean(agg_cols * agg_cols, axis=0, keepdims=True) + eps_norm)
    normed_share = (agg_cols * inverse_norm * gain_column).astype(jnp.bfloat16)
    normed = collect(normed_share, "rel", 1)
    target_pre = lax.dot_general(
        normed, tgt_w_in, (((0,), (0,)), ((), ())), preferred_element_type=jnp.float32
    )
    target_hidden = jax.nn.silu(target_pre).astype(jnp.bfloat16)
    update = summed_on_arrival(
        jnp.dot(target_hidden, tgt_w_out, preferred_element_type=jnp.float32).astype(jnp.bfloat16),
        "rel",
        0,
    )
    updated = (target_feat.astype(jnp.float32) + update).astype(jnp.bfloat16)
    grad_hidden_t = lax.dot_general(
        collect(out_grad, "rel", 0),
        tgt_w_out,
        (((1,), (1,)), ((), ())),
        preferred_element_type=jnp.float32,
    )
    grad_pre_t = (grad_hidden_t * silu_slope(target_pre)).astype(jnp.bfloat16)
    grad_normed = lax.dot_general(
        tgt_w_in, grad_pre_t, (((1,), (1,)), ((), ())), preferred_element_type=jnp.float32
    )
    grad_view = grad_normed.reshape(model_width, relation_count, share_rows)
    grad_part = sent_and_summed(grad_view, "rel", 1).reshape(model_width, share_rows)
    scaled = grad_part * gain_column
    mean_term = jnp.mean(agg_cols * scaled, axis=0, keepdims=True)
    grad_agg = (
        inverse_norm * (scaled - agg_cols * inverse_norm * inverse_norm * mean_term)
    ).astype(jnp.bfloat16)
    spread_share = lax.all_to_all(
        grad_agg.reshape(model_width, 1, share_rows), "dev", split_axis=0, concat_axis=1, tiled=True
    )
    spread_view = spread_share.reshape(feature_width, device_count, 1, share_rows)
    grad_targets = collect(spread_view, "rel", 2).reshape(feature_width, target_total)
    grad_mixed = spread(grad_targets, source_ids, all_counts, source_total).astype(jnp.bfloat16)
    grad_cols = lax.all_to_all(grad_mixed, "dev", split_axis=1, concat_axis=0, tiled=True)
    grad_hidden = lax.dot_general(
        grad_cols, out_full, (((0,), (1,)), ((), ())), preferred_element_type=jnp.float32
    )
    grad_pre = (grad_hidden * silu_slope(hidden_pre)).astype(jnp.bfloat16)
    grad_source = lax.dot_general(
        grad_pre, in_full, (((1,), (1,)), ((), ())), preferred_element_type=jnp.float32
    )
    return (updated, grad_source.astype(jnp.bfloat16)[None])


def solution(mesh):
    placed = (
        P("rel", "dev", None),
        P("rel", "dev", None),
        P("rel", "dev", None),
        P("rel", None),
        P("rel", None, None),
        P("rel", None),
        P(("dev", "rel"), None),
        P(),
        P(None, "rel"),
        P("rel", None),
        P(("dev", "rel"), None),
    )
    return jax.shard_map(
        shards,
        mesh=mesh,
        in_specs=placed,
        out_specs=(P(("dev", "rel"), None), P("rel", "dev", None)),
        check_vma=False,
    )
```

profile of v0, /device:TPU:1, one launch (start us, length us, event | category | flops | bytes accessed | tf_op | source)
XLA Modules:
  0.0 328.1 jit_solution(5152896891152047964)
XLA Ops:
  7.2 1.6 pad_maximum_fusion
  8.8 91.9 %all-gather.2.cloned.1.call-done = bf16[1024,2048]{1,0:T(8,128)(2,1)} async-done(((bf16[32,2048]{1,0:T(8,128)(2,1)}), bf16[1024,2048]{1,0:T(8,128)(2,1)}) %all-gather.2.cloned.1.call-update) | async-done | bytes 4194320 | tf_op jit(solution)/shard_map/all_gather | solution.py:15
  100.8 2.5 fusion.25
  103.6 1.7 fusion.31
  105.2 6.0 %all-to-all-start = ((bf16[32,32,256]{2,1,0:T(8,128)(2,1)}), bf16[32,32,256]{2,1,0:T(8,128)(2,1)S(1)}, u32[]{:S(2)}, u32[]{:S(2)}) async-start(bf16[32,32,256]{2,1,0:T(8,128)(2,1)} %bitcast.19), calls=%async_computation | async-start | bytes 1048576 | tf_op jit(solution)/shard_map/all_to_all | solution.py:152
  111.5 9.0 %fusion.14 = bf16[128,128,128]{2,1,0:T(8,128)(2,1)} fusion(s32[128,128]{1,0:T(8,128)S(1)} %get-tuple-element.288, pred[128,128]{1,0:T(8,128)(4,1)S(1)} %iota_compare_fusion.5, s32[128,128]{1,0:T(8,128)S(1)} %get-tuple-element.287), kind=kOutput, calls=%fused_computation.25 | convolution fusion | flops 545259520 | bytes 4341760 | tf_op jit(solution)/shard_map/kes,ket->kst/dot_general | solution.py:69
  120.5 4.2 %all-to-all-done = bf16[32,32,256]{2,1,0:T(8,128)(2,1)S(1)} async-done(((bf16[32,32,256]{2,1,0:T(8,128)(2,1)}), bf16[32,32,256]{2,1,0:T(8,128)(2,1)S(1)}, u32[]{:S(2)}, u32[]{:S(2)}) %all-to-all-start) | async-done | bytes 524320 | tf_op jit(solution)/shard_map/all_to_all | solution.py:152
  125.1 0.3 copy.46
  125.5 9.9 %while.28 = (s32[]{:T(128)}, f32[32,4096]{1,0:T(8,128)S(1)}, bf16[128,128,128]{2,1,0:T(8,128)(2,1)}, s32[128]{0:T(128)S(1)}, bf16[32,64,128]{2,0,1:T(8,128)(2,1)...) while((s32[]{:T(128)}, f32[32,4096]{1,0:T(8,128)S(1)}, ...), condition=%wide.region_1.2_spmd, body=%wide.region_0.1_spmd.sunk | while | flops 33686728 | bytes 4330325 | solution.py:93
  125.6 0.6 gather_fusion
  126.3 1.3 constant_dynamic-slice_fusion.4
  128.1 0.6 gather_fusion
  128.8 1.3 constant_dynamic-slice_fusion.4
  130.1 0.3 convolution_bitcast_fusion.3
  130.6 0.6 gather_fusion
  131.3 1.3 constant_dynamic-slice_fusion.4
  133.0 0.6 gather_fusion
  133.7 1.3 constant_dynamic-slice_fusion.4
  135.4 0.6 copy.47
  136.0 1.6 copy.75
  137.6 2.5 reshape.379
  140.0 30.1 %all_to_all.92 = f32[16,1,8192]{2,1,0:T(1,128)S(1)} all-to-all(f32[16,1,8192]{2,1,0:T(1,128)S(1)} %reshape.379), channel_id=1, replica_groups=mesh['rel'=16,'dev'=32] {'rel'}, dimensions={0} | all-to-all | bytes 1048576 | tf_op jit(solution)/shard_map/all_to_all | solution.py:30
  170.1 0.5 broadcast.253
  170.6 1.9 reduce.4
  172.6 0.7 reshape.380
  173.5 12.5 %all_to_all.93 = f32[32,1,256]{2,1,0:T(1,128)S(1)} all-to-all(f32[32,1,256]{2,1,0:T(1,128)S(1)} %reshape.381), channel_id=1, replica_groups=mesh['rel'=16,'dev'=32] {'dev'}, dimensions={0} | all-to-all | bytes 65536 | tf_op jit(solution)/shard_map/all_to_all | solution.py:162
  186.1 0.7 reduce.5
  187.3 15.9 %all_to_all.94 = bf16[16,1024,8]{1,2,0:T(8,128)(2,1)S(1)} all-to-all(bf16[16,1024,8]{1,2,0:T(8,128)(2,1)S(1)} %broadcast_in_dim.67), channel_id=1, replica_groups=mesh['rel'=16,'dev'=32] {'rel'}, dimensions={0} | all-to-all | bytes 524288 | tf_op jit(solution)/shard_map/all_to_all | solution.py:42
  203.1 0.7 broadcast_in_dim.69
  203.9 3.4 %all-to-all-start.5 = ((bf16[16,8,1024]{2,1,0:T(8,128)(2,1)}), bf16[16,8,1024]{2,1,0:T(8,128)(2,1)S(1)}, u32[]{:S(2)}, u32[]{:S(2)}) async-start(bf16[16,8,1024]{2,1,0:T(8,128)(2,1)} %broadcast_in_dim.69), calls=%async_computation.5 | async-start | bytes 524288 | tf_op jit(solution)/shard_map/all_to_all | solution.py:42
  207.5 10.9 %all-to-all-done.5 = bf16[16,8,1024]{2,1,0:T(8,128)(2,1)S(1)} async-done(((bf16[16,8,1024]{2,1,0:T(8,128)(2,1)}), bf16[16,8,1024]{2,1,0:T(8,128)(2,1)S(1)}, u32[]{:S(2)}, u32[]{:S(2)}) %all-to-all-start.5) | async-done | bytes 262176 | tf_op jit(solution)/shard_map/all_to_all | solution.py:42
  218.5 1.3 convolution_bitcast_fusion.1
  219.8 3.5 %all-to-all-start.6 = ((f32[16,1024,1,8]{1,3,2,0:T(8,128)}), f32[16,1024,1,8]{1,3,2,0:T(8,128)S(1)}, u32[]{:S(2)}, u32[]{:S(2)}) async-start(f32[16,1024,1,8]{1,3,2,0:T(8,128)} %convolution_bitcast_fusion.1), calls=%async_computation.6 | async-start | bytes 1048576 | tf_op jit(solution)/shard_map/all_to_all | solution.py:30
  223.4 17.0 %all-to-all-done.6 = f32[16,1024,1,8]{1,3,2,0:T(8,128)S(1)} async-done(((f32[16,1024,1,8]{1,3,2,0:T(8,128)}), f32[16,1024,1,8]{1,3,2,0:T(8,128)S(1)}, u32[]{:S(2)}, u32[]{:S(2)}) %all-to-all-start.6) | async-done | bytes 524320 | tf_op jit(solution)/shard_map/all_to_all | solution.py:30
  240.8 0.5 broadcast.255
  241.3 0.7 reduce.6
  242.4 11.6 %all_to_all.95 = bf16[32,2,128]{2,1,0:T(2,128)(2,1)S(1)} all-to-all(bf16[32,2,128]{2,1,0:T(2,128)(2,1)S(1)} %reshape.383), channel_id=1, replica_groups=mesh['rel'=16,'dev'=32] {'dev'}, dimensions={0} | all-to-all | bytes 32768 | tf_op jit(solution)/shard_map/all_to_all | solution.py:195
  254.0 0.7 reshape.384
  255.4 1.7 reshape.385
  257.1 4.0 %all-to-all-start.8 = ((bf16[16,2,4096]{2,1,0:T(2,128)(2,1)}), bf16[16,2,4096]{2,1,0:T(2,128)(2,1)S(1)}, u32[]{:S(2)}, u32[]{:S(2)}) async-start(bf16[16,2,4096]{2,1,0:T(2,128)(2,1)} %reshape.385), calls=%async_computation.8 | async-start | bytes 524288 | tf_op jit(solution)/shard_map/all_to_all | solution.py:42
  261.1 0.9 fusion.47
  262.0 10.7 %all-to-all-done.8 = bf16[16,2,4096]{2,1,0:T(2,128)(2,1)S(1)} async-done(((bf16[16,2,4096]{2,1,0:T(2,128)(2,1)}), bf16[16,2,4096]{2,1,0:T(2,128)(2,1)S(1)}, u32[]{:S(2)}, u32[]{:S(2)}) %all-to-all-start.8) | async-done | bytes 262176 | tf_op jit(solution)/shard_map/all_to_all | solution.py:42
  272.7 4.1 %all-to-all-start.4 = ((bf16[16,8,1024]{2,1,0:T(8,128)(2,1)}), bf16[16,8,1024]{2,1,0:T(8,128)(2,1)}, u32[]{:S(2)}, u32[]{:S(2)}) async-start(bf16[16,8,1024]{2,1,0:T(8,128)(2,1)} %fusion.47), calls=%async_computation.4 | async-start | bytes 524288 | tf_op jit(solution)/shard_map/all_to_all | solution.py:53
  276.8 0.5 reshape.386
  277.6 0.5 copy.57
  278.2 14.9 %while.29 = (s32[]{:T(128)}, f32[32,64,128]{2,0,1:T(8,128)S(1)}, s32[128]{0:T(128)S(1)}, bf16[128,128,128]{2,1,0:T(8,128)(2,1)}, bf16[32,32,128]{2,0,1:T(8,128)(...) while((s32[]{:T(128)}, f32[32,64,128]{2,0,1:T(8,128)S(1)}, s32[128]{0:T(128)S(1)}, ...), condition=%wide.region_9.10_spmd, body=%wide.region_7.9_spmd.sunk | while | flops 33685608 | bytes 5309005 | solution.py:117
  278.3 1.3 constant_dynamic-slice_fusion.5
  279.6 0.4 fusion.92
  280.1 1.9 scatter_fusion
  282.0 1.3 constant_dynamic-slice_fusion.5
  283.3 0.4 fusion.92
  283.8 1.8 scatter_fusion
  285.7 1.3 constant_dynamic-slice_fusion.5
  287.0 0.4 fusion.92
  287.5 1.8 scatter_fusion
  289.4 1.3 constant_dynamic-slice_fusion.5
  290.7 0.4 fusion.92
  291.3 1.8 scatter_fusion
  293.6 1.1 copy.59
  294.7 3.9 %all-to-all-start.9 = ((bf16[32,32,256]{2,0,1:T(8,128)(2,1)}), bf16[32,32,256]{2,0,1:T(8,128)(2,1)S(1)}, u32[]{:S(2)}, u32[]{:S(2)}) async-start(bf16[32,32,256]{2,0,1:T(8,128)(2,1)} %copy.59), calls=%async_computation.9 | async-start | bytes 1048576 | tf_op jit(solution)/shard_map/all_to_all | solution.py:201
  298.6 1.0 convert_reduce_fusion
  299.6 0.6 add_convert_fusion
  300.2 15.7 %all-to-all-done.9 = bf16[32,32,256]{2,0,1:T(8,128)(2,1)S(1)} async-done(((bf16[32,32,256]{2,0,1:T(8,128)(2,1)}), bf16[32,32,256]{2,0,1:T(8,128)(2,1)S(1)}, u32[]{:S(2)}, u32[]{:S(2)}) %all-to-all-start.9) | async-done | bytes 524320 | tf_op jit(solution)/shard_map/all_to_all | solution.py:201
  315.9 5.3 %fusion.42 = bf16[1,256,1024]{2,1,0:T(8,128)(2,1)} fusion(bf16[1024,2048]{1,0:T(8,128)(2,1)} %all-gather.2.cloned.1.call-done, bf16[1024,256]{1,0:T(8,128)(2,1)S(1)} %bitcast.178, f32[256,1024]{0,1:T(8,128)S(1)} %copy-done.11), kind=kOutput, calls=%fused_computation.39 | convolution fusion | flops 1076363264 | bytes 6291456 | tf_op jit(solution)/shard_map/dot_general | solution.py:206
  (84 shorter events, 6.6 us)
Async XLA Ops:
  7.2 93.6 %copy-start = (bf16[1,256,1024]{2,1,0:T(8,128)(2,1)S(1)}, bf16[1,256,1024]{2,1,0:T(8,128)(2,1)}, u32[]{:S(2)}) copy-start(bf16[1,256,1024]{2,1,0:T(8,128)(2,1)} %param.15) | copy-start | bytes 1572868
  7.2 93.6 %all-gather.2.cloned.1.call-start = ((), (), s32[]{:S(2)}) async-start(), calls=%async_computation.10 | async-start | bytes 4325376 | tf_op jit(solution)/shard_map/all_gather | solution.py:15
  100.7 2.8 copy-start.9
  103.6 1.7 copy-start.10
  103.6 7.7 %copy-start.8 = (s32[1,128]{1,0:T(1,128)S(1)}, s32[1,128]{1,0:T(1,128)}, u32[]{:S(2)}) copy-start(s32[1,128]{1,0:T(1,128)} %param.20) | copy-start | bytes 1540
  103.6 7.8 %copy-start.3 = (s32[1,128,128]{2,1,0:T(8,128)S(1)}, s32[1,128,128]{2,1,0:T(8,128)}, u32[]{:S(2)}) copy-start(s32[1,128,128]{2,1,0:T(8,128)} %param.19) | copy-start | bytes 196612
  105.2 19.4 %all-to-all-start = ((bf16[32,32,256]{2,1,0:T(8,128)(2,1)}), bf16[32,32,256]{2,1,0:T(8,128)(2,1)S(1)}, u32[]{:S(2)}, u32[]{:S(2)}) async-start(bf16[32,32,256]{2,1,0:T(8,128)(2,1)} %bitcast.19), calls=%async_computation | async-start | bytes 1048576 | tf_op jit(solution)/shard_map/all_to_all | solution.py:152
  111.5 14.0 %copy-start.7 = (s32[1,128]{1,0:T(1,128)S(1)}, s32[1,128]{1,0:T(1,128)}, u32[]{:S(2)}) copy-start(s32[1,128]{1,0:T(1,128)} %param.18) | copy-start | bytes 1540
  140.0 47.2 %copy-start.4 = (f32[1024]{0:T(1024)S(1)}, f32[1024]{0:T(1024)}, u32[]{:S(2)}) copy-start(f32[1024]{0:T(1024)} %param.22) | copy-start | bytes 12292
  170.1 33.0 %copy-start.5 = (bf16[8,1024]{1,0:T(8,128)(2,1)S(1)}, bf16[8,1024]{1,0:T(8,128)(2,1)}, u32[]{:S(2)}) copy-start(bf16[8,1024]{1,0:T(8,128)(2,1)} %param.25) | copy-start | bytes 49156
  170.6 36.7 %copy-start.1 = (bf16[1024,128]{1,0:T(8,128)(2,1)S(1)}, bf16[1024,128]{1,0:T(8,128)(2,1)}, u32[]{:S(2)}) copy-start(bf16[1024,128]{1,0:T(8,128)(2,1)} %param.23) | copy-start | bytes 786436
  173.2 45.2 %copy-start.2 = (bf16[128,1024]{1,0:T(8,128)(2,1)S(1)}, bf16[128,1024]{1,0:T(8,128)(2,1)}, u32[]{:S(2)}) copy-start(bf16[128,1024]{1,0:T(8,128)(2,1)} %param.24) | copy-start | bytes 786436
  203.9 14.6 %all-to-all-start.5 = ((bf16[16,8,1024]{2,1,0:T(8,128)(2,1)}), bf16[16,8,1024]{2,1,0:T(8,128)(2,1)S(1)}, u32[]{:S(2)}, u32[]{:S(2)}) async-start(bf16[16,8,1024]{2,1,0:T(8,128)(2,1)} %broadcast_in_dim.69), calls=%async_computation.5 | async-start | bytes 524288 | tf_op jit(solution)/shard_map/all_to_all | solution.py:42
  219.8 20.6 %all-to-all-start.6 = ((f32[16,1024,1,8]{1,3,2,0:T(8,128)}), f32[16,1024,1,8]{1,3,2,0:T(8,128)S(1)}, u32[]{:S(2)}, u32[]{:S(2)}) async-start(f32[16,1024,1,8]{1,3,2,0:T(8,128)} %convolution_bitcast_fusion.1), calls=%async_computation.6 | async-start | bytes 1048576 | tf_op jit(solution)/shard_map/all_to_all | solution.py:30
  257.1 15.6 %all-to-all-start.8 = ((bf16[16,2,4096]{2,1,0:T(2,128)(2,1)}), bf16[16,2,4096]{2,1,0:T(2,128)(2,1)S(1)}, u32[]{:S(2)}, u32[]{:S(2)}) async-start(bf16[16,2,4096]{2,1,0:T(2,128)(2,1)} %reshape.385), calls=%async_computation.8 | async-start | bytes 524288 | tf_op jit(solution)/shard_map/all_to_all | solution.py:42
  272.7 22.0 %all-to-all-start.4 = ((bf16[16,8,1024]{2,1,0:T(8,128)(2,1)}), bf16[16,8,1024]{2,1,0:T(8,128)(2,1)}, u32[]{:S(2)}, u32[]{:S(2)}) async-start(bf16[16,8,1024]{2,1,0:T(8,128)(2,1)} %fusion.47), calls=%async_computation.4 | async-start | bytes 524288 | tf_op jit(solution)/shard_map/all_to_all | solution.py:53
  293.1 6.5 %copy-start.6 = (bf16[8,1024]{1,0:T(8,128)(2,1)S(1)}, bf16[8,1024]{1,0:T(8,128)(2,1)}, u32[]{:S(2)}) copy-start(bf16[8,1024]{1,0:T(8,128)(2,1)} %param.21) | copy-start | bytes 49156
  293.1 22.8 %copy-start.11 = (f32[256,1024]{0,1:T(8,128)S(1)}, f32[256,1024]{0,1:T(8,128)}, u32[]{:S(2)}) copy-start(f32[256,1024]{0,1:T(8,128)} %copy-done.10) | copy-start | bytes 3145732
  294.7 21.2 %all-to-all-start.9 = ((bf16[32,32,256]{2,0,1:T(8,128)(2,1)}), bf16[32,32,256]{2,0,1:T(8,128)(2,1)S(1)}, u32[]{:S(2)}, u32[]{:S(2)}) async-start(bf16[32,32,256]{2,0,1:T(8,128)(2,1)} %copy.59), calls=%async_computation.9 | async-start | bytes 1048576 | tf_op jit(solution)/shard_map/all_to_all | solution.py:201
Sparse Core Ops, SparseCore 0:
  11.7 88.9 all-gather.1
where the time goes:
time: 329 us; the launch traced here: 328 us
  waiting for transfers between devices  150 us (46%)
  blocking collectives  70 us (21%)
  local copies, waits for them, and re-layouts  28.5 us (9%)
  starting transfers between devices  25 us (8%)
  matrix products  24 us (7%)
  other arithmetic  15.4 us (5%)
  between operations  14.4 us (4%)
    all_gather x1, waiting for transfers between devices, in_one_piece(): lax.all_gather(both, axis, axis=dim, tiled=True)  91.9 us
    all_to_all x1, blocking collectives, sent_and_summed(): lax.all_to_all(parts, axis, split_axis=0, concat_axis=0, tiled=True)  30.1 us
    all_to_all x2, waiting for transfers between devices, from_everyone(): lax.all_to_all(jnp.broadcast_to(array[None], (length, *array.shape)), axi...  21.6 us
    all_to_all x1, waiting for transfers between devices, sent_and_summed(): lax.all_to_all(parts, axis, split_axis=0, concat_axis=0, tiled=True)  17 us
    all_to_all x1, blocking collectives, from_everyone(): lax.all_to_all(jnp.broadcast_to(array[None], (length, *array.shape)), axi...  15.9 us
    all_to_all x1, waiting for transfers between devices, shards(): lax.all_to_all(grad_mixed, 'dev', split_axis=1, concat_axis=0, tiled=True)  15.7 us
    all_to_all x1, blocking collectives, shards(): lax.all_to_all(shared_sum, 'dev', split_axis=1, concat_axis=0, tiled=True)  12.5 us
    all_to_all x1, blocking collectives, shards(): lax.all_to_all(grad_agg.reshape(model_width, 1, share_rows), 'dev', split...  11.6 us
  transfers between devices with their start and end apart: 7, of which 6 were waited for; matrix products, arithmetic and copies ran while one was open for 9% of the time, Pallas kernels for 0%

commit v1 on v0

v1 whole, which is shorter than its diff:
```python
import functools

import jax
import jax.numpy as jnp
from jax import lax
from jax.experimental import pallas as pl
from jax.experimental.pallas import tpu as pltpu
from jax.sharding import PartitionSpec as P

TILE = 128
TILE_ROW = 4
RING_X = 4

eps_norm = 1e-06

BF = jnp.bfloat16
F32 = jnp.float32
MESH = pl.DeviceIdType.MESH


def silu_slope(values):
    sigma = jax.nn.sigmoid(values)
    return sigma * (1.0 + values * (1.0 - sigma))


def dot_nn(a, b):
    return lax.dot_general(a, b, (((1,), (0,)), ((), ())), preferred_element_type=F32)


def dot_nt(a, b):
    return lax.dot_general(a, b, (((1,), (1,)), ((), ())), preferred_element_type=F32)


def tile_tables(source_ids, source_blocks):
    total = source_ids.shape[0]
    spot = jnp.arange(total, dtype=jnp.int32)
    earlier = (source_ids[None, :] < source_ids[:, None]) | (
        (source_ids[None, :] == source_ids[:, None]) & (spot[None, :] < spot[:, None])
    )
    rank = jnp.sum(earlier.astype(jnp.int32), axis=1)
    placed = rank[:, None] == spot[None, :]
    order = jnp.sum(jnp.where(placed, spot[:, None], 0), axis=0)
    here = jnp.sum(jnp.where(placed, source_ids[:, None], 0), axis=0)
    before = jnp.sum(jnp.where(rank[:, None] + 1 == spot[None, :], source_ids[:, None] + 1, 0), axis=0) - 1
    keep = (here == before).astype(jnp.int32)
    named = source_ids[:, None] == spot[None, :]
    upto = jnp.sum((source_ids[:, None] <= spot[None, :]).astype(jnp.int32), axis=0)
    last = jnp.where(jnp.any(named, axis=0), upto - 1, total)
    return jnp.stack([order, order // TILE_ROW, keep, last])


def whole_kernel(
    DV,
    R,
    ids,
    live,
    tab,
    src,
    win,
    wout,
    edges,
    tfeat,
    gain,
    twi,
    two,
    og,
    upd_out,
    grad_out,
    w_in,
    w_out,
    pre,
    hid_t,
    hid_by_feature,
    counts,
    agg_send,
    agg_recv,
    part_send,
    part_recv,
    norm_send,
    norm_recv,
    og_send,
    og_recv,
    gn_send,
    gn_recv,
    up_send,
    up_recv,
    ga_send,
    ga_recv,
    gt_send,
    gt_recv,
    runs,
    gh_send,
    gh_recv,
    grad_pre,
    ring_sem,
    ring_send_sem,
    send_sem,
    recv_sem,
):
    D = src.shape[1]
    half_d = D // 2
    F = D // DV
    H = F // 2
    T = ids.shape[1]
    TR = tfeat.shape[0]
    X = RING_X
    Y = DV // X
    HY = Y // 2
    W = min(256, half_d)
    rd = lax.axis_index("rel")
    me = lax.axis_index("dev")
    my_y = me // X
    my_x = lax.rem(me, X)

    def at(dy, dx):
        return lax.rem(my_y + dy + Y, Y) * X + lax.rem(my_x + dx + X, X)

    barrier = pltpu.get_barrier_semaphore()

    def greet_dev(i, c):
        pl.semaphore_signal(
            barrier, inc=1, device_id={"dev": lax.rem(me + i, DV)}, device_id_type=MESH
        )
        return c

    def greet_rel(i, c):
        pl.semaphore_signal(
            barrier, inc=1, device_id={"rel": lax.rem(rd + i, R)}, device_id_type=MESH
        )
        return c

    lax.fori_loop(1, DV, greet_dev, 0)
    lax.fori_loop(1, R, greet_rel, 0)
    pl.semaphore_wait(barrier, DV + R - 2)

    full = (w_in, w_out)
    own = (win, wout)

    def rows_of(block, half):
        return pl.ds(pl.multiple_of(block * F + half * H, H), H)

    def push(w, half, block, to, own_block=False):
        rows = rows_of(block, half)
        piece = own[w].at[pl.ds(half * H, H)] if own_block else full[w].at[rows]
        pltpu.make_async_remote_copy(
            src_ref=piece,
            dst_ref=full[w].at[rows],
            send_sem=ring_send_sem.at[w],
            recv_sem=ring_sem.at[w, half, block],
            device_id={"dev": to},
            device_id_type=MESH,
        ).start()

    def arrive(w, half, block):
        piece = full[w].at[rows_of(block, half)]
        pltpu.make_async_copy(piece, piece, ring_sem.at[w, half, block]).wait()

    def begin(w):
        push(w, 0, me, at(1, 0), True)
        push(w, 0, me, at(-1, 0), True)
        push(w, 1, me, at(0, 1), True)
        push(w, 1, me, at(0, -1), True)
        push(w, 0, me, at(0, 1), True)
        push(w, 0, me, at(0, -1), True)
        push(w, 1, me, at(1, 0), True)
        push(w, 1, me, at(-1, 0), True)
        push(w, 0, me, at(0, 2), True)
        full[w][pl.ds(pl.multiple_of(me * F, F), F), :] = own[w][...]

    def relay_x(w, dy):
        y = lax.rem(my_y + dy + Y, Y)
        even = lax.rem(y, 2) == 0
        arrive(w, 1, at(dy, -1))
        arrive(w, 1, at(dy, 1))
        block = jnp.where(even, at(dy, -1), at(dy, 1))
        push(w, 1, block, jnp.where(even, at(0, 1), at(0, -1)))

    def round_of(w, s):
        if s <= HY:

            def column(i, c):
                dx = lax.rem(i * 3, X)
                if s == 0:
                    arrive(w, 0, at(0, dx))
                    push(w, 0, at(0, dx), at(1, 0))
                    push(w, 0, at(0, dx), at(-1, 0))
                elif s < HY:
                    arrive(w, 0, at(-s, dx))
                    if s < HY - 1:
                        push(w, 0, at(-s, dx), at(1, 0))
                    arrive(w, 0, at(s, dx))
                    if s < HY - 1:
                        push(w, 0, at(s, dx), at(-1, 0))
                    else:
                        even = lax.rem(my_x + dx, 2) == 0
                        push(
                            w,
                            0,
                            jnp.where(even, at(-s, dx), at(s, dx)),
                            jnp.where(even, at(1, 0), at(-1, 0)),
                        )
                else:
                    arrive(w, 0, at(HY, dx))
                return c

            lax.fori_loop(1 if s == 0 else 0, X, column, 0)
        if 1 <= s < HY:
            for d in (-s, s):
                arrive(w, 1, at(d, 0))
                if s < HY - 1:
                    push(w, 1, at(d, 0), at(1 if d < 0 else -1, 0))
                push(w, 1, at(d, 0), at(0, 1))
                push(w, 1, at(d, 0), at(0, -1))
            if s == HY - 1:
                even = lax.rem(my_x, 2) == 0
                push(
                    w,
                    1,
                    jnp.where(even, at(-s, 0), at(s, 0)),
                    jnp.where(even, at(1, 0), at(-1, 0)),
                )
        elif s == HY:
            arrive(w, 1, at(HY, 0))
            push(w, 1, at(HY, 0), at(0, 1))
            push(w, 1, at(HY, 0), at(0, -1))
        if s == 1:
            relay_x(w, 0)
        elif 2 <= s <= HY:
            relay_x(w, -(s - 1))
            relay_x(w, s - 1)
        elif s == HY + 1:
            relay_x(w, HY)
        if s == HY + 1:

            def rest(i, c):
                arrive(w, 1, i * X + lax.rem(my_x + 2, X))
                return c

            lax.fori_loop(0, Y, rest, 0)

    ROUNDS = HY + 2

    def over_dev(n, piece, place):
        def send(i, c):
            to = lax.rem(me + i, DV)
            pltpu.make_async_remote_copy(
                src_ref=piece(to),
                dst_ref=place,
                send_sem=send_sem.at[n],
                recv_sem=recv_sem.at[n],
                device_id={"dev": to},
                device_id_type=MESH,
            ).start()
            return c

        lax.fori_loop(1, DV, send, 0)

    def over_rel(n, piece, place):
        def send(i, c):
            to = lax.rem(rd + i, R)
            pltpu.make_async_remote_copy(
                src_ref=piece(to),
                dst_ref=place,
                send_sem=send_sem.at[n],
                recv_sem=recv_sem.at[n],
                device_id={"rel": to},
                device_id_type=MESH,
            ).start()
            return c

        lax.fori_loop(1, R, send, 0)

    def all_of(sem, view):
        pltpu.make_async_copy(view, view, sem).wait()

    def folded(rows):
        return jnp.concatenate([rows[..., :half_d], rows[..., half_d:]], axis=-2).astype(BF)

    def block_rows(buffer):
        held = buffer[...].astype(F32)
        rows = jnp.concatenate([held[:, :TR, :], held[:, TR:, :]], axis=2)
        return rows.reshape(R * TR, D).astype(BF)

    def own_sum(buffer):
        total = buffer[0].astype(F32)
        for r in range(1, R):
            total = total + buffer[r].astype(F32)
        return jnp.concatenate([total[:TR], total[TR:]], axis=1)

    def count_tiles(first, number):
        lattice = lax.broadcasted_iota(jnp.int32, (TILE, TILE), 0)
        slots = lax.broadcasted_iota(jnp.int32, (1, TILE), 1)

        def some(i, c):
            for u in range(4):
                k = first + i * 4 + u
                codes = edges[pl.ds(k, 1), :]
                s_at = jnp.bitwise_and(codes, TILE - 1)
                t_at = jnp.where(slots < live[0, k], jnp.right_shift(codes, 7), -1)
                s_hot = (lattice == s_at).astype(F32).astype(BF)
                t_hot = (lattice == t_at).astype(F32).astype(BF)
                counts[k] = dot_nt(s_hot, t_hot).astype(BF)
            return c

        lax.fori_loop(0, number // 4, some, 0)

    begin(0)
    og_send[...] = folded(og[...].astype(F32))
    og_recv[rd] = og_send[...]
    over_rel(0, lambda to: og_send, og_recv.at[rd])
    share = T // 8
    for s in range(ROUNDS):
        count_tiles(s * share, share)
        round_of(0, s)
    begin(1)

    def first_projection(j, c):
        cols = pl.ds(pl.multiple_of(j * W, W), W)
        value = dot_nn(src[...], w_in[:, cols])
        pre[:, cols] = value
        turned = (value * jax.nn.sigmoid(value)).T.astype(BF)
        hid_t[0, cols, :] = turned[:, :TILE]
        hid_t[1, cols, :] = turned[:, TILE:]
        return c

    lax.fori_loop(0, D // W, first_projection, 0)
    over_dev(
        1,
        lambda to: hid_t.at[:, pl.ds(pl.multiple_of(to * F, F), F), :],
        hid_by_feature.at[pl.ds(2 * me, 2)],
    )
    hid_by_feature[pl.ds(2 * me, 2)] = hid_t[:, pl.ds(pl.multiple_of(me * F, F), F), :]
    early = HY
    for s in range(early):
        if s == 0:
            count_tiles(ROUNDS * share, T - ROUNDS * share)
        round_of(1, s)
    all_of(recv_sem.at[0], og_recv.at[pl.ds(0, R - 1)])
    grad_hidden_t = dot_nt(block_rows(og_recv), two[...])

    all_of(recv_sem.at[1], hid_by_feature.at[pl.ds(0, 2 * (DV - 1))])

    def aggregate(i, c):
        for u in range(4):
            b = i * 4 + u
            total = jnp.zeros((F, TILE), F32)
            for q in range(TILE_ROW):
                k = b * TILE_ROW + q
                total = total + dot_nn(hid_by_feature[ids[0, k]], counts[k])
            agg_send[b] = total.astype(BF)
        return c

    lax.fori_loop(0, T // TILE_ROW // 4, aggregate, 0)
    my_rows = pl.ds(pl.multiple_of(me * F, F), F)
    over_dev(2, lambda to: agg_send.at[to], agg_recv.at[my_rows])
    agg_recv[my_rows, :] = agg_send[me]
    for s in range(early, ROUNDS):
        round_of(1, s)
    all_of(recv_sem.at[2], agg_recv.at[pl.ds(0, D - F)])

    agg_hidden = agg_recv[...].astype(F32).T.astype(BF)
    for j in range(half_d // W):
        low = dot_nn(agg_hidden, w_out[:, j * W : (j + 1) * W])
        high = dot_nn(agg_hidden, w_out[:, half_d + j * W : half_d + (j + 1) * W])
        both = jnp.concatenate([low.reshape(R, TR, W), high.reshape(R, TR, W)], axis=1)
        part_send[:, :, j * W : (j + 1) * W] = both.astype(BF)
    over_rel(3, lambda to: part_send.at[to], part_recv.at[rd])
    part_recv[rd] = part_send[rd]
    all_of(recv_sem.at[3], part_recv.at[pl.ds(0, R - 1)])
    agg = own_sum(part_recv)
    gain_row = gain[...]
    inverse_norm = lax.rsqrt(jnp.mean(agg * agg, axis=1, keepdims=True) + eps_norm)
    norm_send[...] = folded(agg * inverse_norm * gain_row)
    over_rel(4, lambda to: norm_send, norm_recv.at[rd])
    norm_recv[rd] = norm_send[...]
    all_of(recv_sem.at[4], norm_recv.at[pl.ds(0, R - 1)])
    target_pre = dot_nn(block_rows(norm_recv), twi[...])
    grad_pre_t = (grad_hidden_t * silu_slope(target_pre)).astype(BF)
    gn_send[...] = folded(dot_nt(grad_pre_t, twi[...]).reshape(R, TR, D))
    over_rel(5, lambda to: gn_send.at[to], gn_recv.at[rd])
    gn_recv[rd] = gn_send[rd]
    target_hidden = (target_pre * jax.nn.sigmoid(target_pre)).astype(BF)
    up_send[...] = folded(dot_nn(target_hidden, two[...]).reshape(R, TR, D))
    all_of(recv_sem.at[5], gn_recv.at[pl.ds(0, R - 1)])
    scaled = own_sum(gn_recv) * gain_row
    mean_term = jnp.mean(agg * scaled, axis=1, keepdims=True)
    ga_send[...] = folded(
        inverse_norm * (scaled - agg * inverse_norm * inverse_norm * mean_term)
    )
    over_rel(7, lambda to: ga_send, ga_recv.at[rd])
    over_rel(6, lambda to: up_send.at[to], up_recv.at[rd])
    ga_recv[rd] = ga_send[...]
    up_recv[rd] = up_send[rd]
    all_of(recv_sem.at[7], ga_recv.at[pl.ds(0, R - 1)])

    grad_agg = block_rows(ga_recv)
    for j in range(D // W):
        value = dot_nt(grad_agg, w_out[j * W : (j + 1) * W, :])
        gt_send[j * W : (j + 1) * W, :] = value.T.astype(BF)
    over_dev(
        8, lambda to: gt_send.at[pl.ds(pl.multiple_of(to * F, F), F)], gt_recv.at[me]
    )
    gt_recv[me] = gt_send[my_rows, :]
    runs[T] = jnp.zeros((F, TILE), F32)
    all_of(recv_sem.at[8], gt_recv.at[pl.ds(0, DV - 1)])

    def spread(i, running):
        for u in range(8):
            j = i * 8 + u
            term = dot_nt(gt_recv[tab[1, j]], counts[tab[0, j]])
            running = running * tab[2, j].astype(F32) + term
            runs[j] = running
        return running

    lax.fori_loop(0, T // 8, spread, jnp.zeros((F, TILE), F32))

    def settle(i, c):
        for u in range(8):
            b = i * 8 + u
            gh_send[b] = runs[tab[3, b]].astype(BF)
        return c

    lax.fori_loop(0, 2 * DV // 8, settle, 0)
    over_dev(9, lambda to: gh_send.at[pl.ds(2 * to, 2)], gh_recv.at[:, my_rows, :])
    gh_recv[:, my_rows, :] = gh_send[pl.ds(2 * me, 2)]

    all_of(recv_sem.at[6], up_recv.at[pl.ds(0, R - 1)])
    upd_out[...] = (tfeat[...].astype(F32) + own_sum(up_recv)).astype(BF)
    for w in range(2):
        all_of(ring_send_sem.at[w], full[w].at[pl.ds(0, D - F)])
    all_of(send_sem.at[1], hid_by_feature.at[pl.ds(0, 2 * (DV - 1))])
    all_of(send_sem.at[2], agg_recv.at[pl.ds(0, D - F)])
    for n, held in (
        (0, og_recv),
        (3, part_recv),
        (4, norm_recv),
        (5, gn_recv),
        (6, up_recv),
        (7, ga_recv),
    ):
        all_of(send_sem.at[n], held.at[pl.ds(0, R - 1)])
    all_of(send_sem.at[8], gt_recv.at[pl.ds(0, DV - 1)])

    all_of(recv_sem.at[9], gh_recv.at[:, pl.ds(0, D - F), :])

    def last_slope(j, c):
        cols = pl.ds(pl.multiple_of(j * W, W), W)
        turned = jnp.concatenate([gh_recv[0, cols, :], gh_recv[1, cols, :]], axis=1)
        value = turned.astype(F32).T * silu_slope(pre[:, cols])
        grad_pre[:, cols] = value.astype(BF)
        return c

    lax.fori_loop(0, D // W, last_slope, 0)

    def last_projection(j, c):
        cols = pl.ds(pl.multiple_of(j * W, W), W)
        grad_out[:, cols] = dot_nt(grad_pre[...], w_in[cols, :]).astype(BF)
        return c

    lax.fori_loop(0, D // W, last_projection, 0)
    all_of(send_sem.at[9], gh_recv.at[:, pl.ds(0, D - F), :])


def shards(
    src_feat,
    rel_w_in,
    rel_w_out,
    tile_source,
    tile_edges,
    tile_count,
    target_feat,
    norm_gain,
    tgt_w_in,
    tgt_w_out,
    out_grad,
):
    DV = lax.axis_size("dev")
    R = lax.axis_size("rel")
    own_rows = src_feat[0]
    rows, D = own_rows.shape
    F = D // DV
    T = tile_source.shape[1]
    TR = target_feat.shape[0]
    tables = tile_tables(tile_source[0], rows * DV // TILE)

    vmem = pl.BlockSpec(memory_space=pltpu.VMEM)
    smem = pl.BlockSpec(memory_space=pltpu.SMEM)
    piece = pltpu.VMEM((2 * TR, D // 2), BF)
    pieces = pltpu.VMEM((R, 2 * TR, D // 2), BF)
    updated, grad_source = pl.pallas_call(
        functools.partial(whole_kernel, DV, R),
        out_shape=(
            jax.ShapeDtypeStruct((TR, D), BF),
            jax.ShapeDtypeStruct((rows, D), BF),
        ),
        in_specs=[smem] * 3 + [vmem] * 9,
        out_specs=(vmem, vmem),
        scratch_shapes=[
            pltpu.VMEM((D, D), BF),
            pltpu.VMEM((D, D), BF),
            pltpu.VMEM((rows, D), F32),
            pltpu.VMEM((2, D, TILE), BF),
            pltpu.VMEM((2 * DV, F, TILE), BF),
            pltpu.VMEM((T, TILE, TILE), BF),
            pltpu.VMEM((DV, F, TILE), BF),
            pltpu.VMEM((D, TILE), BF),
            pieces,
            pieces,
            piece,
            pieces,
            piece,
            pieces,
            pieces,
            pieces,
            pieces,
            pieces,
            piece,
            pieces,
            pltpu.VMEM((D, TILE), BF),
            pltpu.VMEM((DV, F, TILE), BF),
            pltpu.VMEM((T + 1, F, TILE), F32),
            pltpu.VMEM((2 * DV, F, TILE), BF),
            pltpu.VMEM((2, D, TILE), BF),
            pltpu.VMEM((rows, D), BF),
            pltpu.SemaphoreType.DMA((2, 2, DV)),
            pltpu.SemaphoreType.DMA((2,)),
            pltpu.SemaphoreType.DMA((10,)),
            pltpu.SemaphoreType.DMA((10,)),
        ],
        compiler_params=pltpu.CompilerParams(
            collective_id=0, has_side_effects=True, vmem_limit_bytes=60 * 1024 * 1024
        ),
        name="whole_layer",
    )(
        tile_source,
        tile_count,
        tables,
        own_rows,
        rel_w_in[0],
        rel_w_out[0],
        tile_edges[0],
        target_feat,
        norm_gain[None, :],
        tgt_w_in,
        tgt_w_out,
        out_grad,
    )
    return (updated, grad_source[None])


def solution(mesh):
    placed = (
        P("rel", "dev", None),
        P("rel", "dev", None),
        P("rel", "dev", None),
        P("rel", None),
        P("rel", None, None),
        P("rel", None),
        P(("dev", "rel"), None),
        P(),
        P(None, "rel"),
        P("rel", None),
        P(("dev", "rel"), None),
    )
    return jax.shard_map(
        shards,
        mesh=mesh,
        in_specs=placed,
        out_specs=(P(("dev", "rel"), None), P("rel", "dev", None)),
        check_vma=False,
    )
```

time: 329 us -> 153 us (0.47)
  waiting for transfers between devices: 150 us -> 0 us
  Pallas kernels: 0 us -> 145 us
  blocking collectives: 70 us -> 0 us
  starting transfers between devices: 25 us -> 0 us
  local copies, waits for them, and re-layouts: 28.5 us -> 3.84 us
  matrix products: 24 us -> 0 us
  other arithmetic: 15.4 us -> 1.12 us
  between operations: 14.4 us -> 0.68 us
    pallas_call x0 -> x1, Pallas kernels: none -> 145 us  [shards(): pl.pallas_call(functools.partial(whole_kernel, DV, R), out_shape=(jax.Sha...]
    all_gather x1 -> x0, waiting for transfers between devices: 91.9 us -> none  [in_one_piece(): lax.all_gather(both, axis, axis=dim, tiled=True)]
    all_to_all x4 -> x0, blocking collectives: 70 us -> none  [the longest x1 30.1 us: sent_and_summed(): lax.all_to_all(parts, axis, split_axis=0, concat_axis=0, tiled=True)]
    all_to_all x6 -> x0, waiting for transfers between devices: 58.4 us -> none  [the longest x2 21.6 us: from_everyone(): lax.all_to_all(jnp.broadcast_to(array[None], (length, *array.shape)), axi...]
    all_to_all x6 -> x0, starting transfers between devices: 25 us -> none  [the longest x2 7.48 us: from_everyone(): lax.all_to_all(jnp.broadcast_to(array[None], (length, *array.shape)), axi...]
    dot_general x15 -> x0, matrix products: 24 us -> none  [the longest x1 9 us: tile_counts(): jnp.einsum('kes,ket->kst', source_hot, target_hot, preferred_element_type...]
    dynamic_slice x8 -> x0, local copies, waits for them, and re-layouts: 10.4 us -> none  [the longest x4 5.19 us: aggregate_advance(): lax.dynamic_slice_in_dim(all_counts, offset, per_turn, 0)]
    scatter-add x4 -> x0, other arithmetic: 7.38 us -> none  [spread_advance(): return running.at[:, chosen, :].add(pieces)]
  transfers between devices with their start and end apart: 7 -> 0, of which waited for: 6 -> 0; matrix products, arithmetic and copies ran while one was open for 9% -> 0% of each run, Pallas kernels for 0% -> 0%
where the time goes in v1:
time: 153 us; the launch traced here: 151 us
  Pallas kernels  145 us (95%)
  local copies, waits for them, and re-layouts  3.84 us (3%)
    pallas_call x1, Pallas kernels, shards(): pl.pallas_call(functools.partial(whole_kernel, DV, R), out_shape=(jax.Sha...  145 us
    unnamed x4, local copies, waits for them, and re-layouts  3.84 us

profile of v1, /device:TPU:1, one launch (start us, length us, event | category | flops | bytes accessed | tf_op | source)
XLA Modules:
  0.0 150.5 jit_solution(508998876124304743)
XLA Ops:
  0.6 0.0 copy-start
  0.6 0.6 copy-done
  1.3 0.2 convert_reduce_fusion.1
  1.5 0.1 fusion.2
  1.6 0.1 select_reduce_fusion
  1.7 0.1 select_reduce_fusion.2
  1.9 0.6 pad_add_fusion.tab
  2.4 144.9 %whole_layer.1 = (bf16[8,1024]{1,0:T(8,128)(2,1)}, bf16[256,1024]{1,0:T(8,128)(2,1)}) custom-call(s32[1,128]{1,0:T(1,128)} %ids.1, s32[1,128]{1,0:T(1,128)} %live.1, s32[4,128]{1,0:T(4,128)} %pad_add_fusion.tab, bf16[256,1024]{1,0:T(8,128)(2,1)} %bitcast.14, bf16[32,1024]{1,0:T(8,128)(2,1)} %bitcast.16, bf16[32,1024]{1,0:T(8,128)(2,1)} %bitcast.17, ...), custom_call_target="tpu_custom_call" | custom-call | tf_op jit(solution)/shard_map/whole_layer/pallas_call | solution.py:490
  147.3 1.3 copy.15
  148.7 1.9 %copy.16 = bf16[1,256,1024]{2,1,0:T(8,128)(2,1)} copy(bf16[1,256,1024]{2,1,0:T(8,128)(2,1)} %bitcast.15) | data formatting | bytes 1048576
  (4 shorter events, 0.0 us)
Async XLA Ops:
  0.6 0.7 copy-start

commit v2 on v1

v2 whole, which is shorter than its diff:
```python
import functools

import jax
import jax.numpy as jnp
from jax import lax
from jax.experimental import pallas as pl
from jax.experimental.pallas import tpu as pltpu
from jax.sharding import PartitionSpec as P

TILE = 128
TILE_ROW = 4
RING_X = 4

eps_norm = 1e-06

BF = jnp.bfloat16
F32 = jnp.float32
MESH = pl.DeviceIdType.MESH


def silu_slope(values):
    sigma = jax.nn.sigmoid(values)
    return sigma * (1.0 + values * (1.0 - sigma))


def dot_nn(a, b):
    return lax.dot_general(a, b, (((1,), (0,)), ((), ())), preferred_element_type=F32)


def dot_nt(a, b):
    return lax.dot_general(a, b, (((1,), (1,)), ((), ())), preferred_element_type=F32)


def tile_tables(source_ids, source_blocks):
    total = source_ids.shape[0]
    spot = jnp.arange(total, dtype=jnp.int32)
    earlier = (source_ids[None, :] < source_ids[:, None]) | (
        (source_ids[None, :] == source_ids[:, None]) & (spot[None, :] < spot[:, None])
    )
    rank = jnp.sum(earlier.astype(jnp.int32), axis=1)
    placed = rank[:, None] == spot[None, :]
    order = jnp.sum(jnp.where(placed, spot[:, None], 0), axis=0)
    here = jnp.sum(jnp.where(placed, source_ids[:, None], 0), axis=0)
    before = jnp.sum(jnp.where(rank[:, None] + 1 == spot[None, :], source_ids[:, None] + 1, 0), axis=0) - 1
    keep = (here == before).astype(jnp.int32)
    named = source_ids[:, None] == spot[None, :]
    upto = jnp.sum((source_ids[:, None] <= spot[None, :]).astype(jnp.int32), axis=0)
    last = jnp.where(jnp.any(named, axis=0), upto - 1, total)
    return jnp.stack([order, order // TILE_ROW, keep, last])


def whole_kernel(
    DV,
    R,
    ids,
    live,
    tab,
    src_in,
    win_in,
    wout_in,
    edges_in,
    tfeat,
    gain,
    twi_in,
    two_in,
    og,
    upd_out,
    grad_out,
    src,
    edges,
    w_a,
    w_b,
    w_out,
    twi,
    two,
    pre,
    hid_t,
    hid_by_feature,
    counts,
    agg_send,
    agg_recv,
    part_send,
    part_pair,
    part_sum,
    part_recv,
    ga_send,
    ga_recv,
    gt_send,
    gt_recv,
    runs,
    gh_send,
    gh_recv,
    grad_pre,
    copy_sem,
    ring_sem,
    ring_send_sem,
    y_sem,
    x_sem,
    far_sem,
    wout_send_sem,
    z_sem,
    z_send_sem,
    ga_sem,
    send_sem,
    recv_sem,
):
    D = src.shape[1]
    HD = D // 2
    F = D // DV
    T = ids.shape[1]
    TR = tfeat.shape[0]
    X = RING_X
    Y = DV // X
    HY = Y // 2
    Z = R // 2
    HZ = Z // 2
    W = min(256, HD)
    rd = lax.axis_index("rel")
    me = lax.axis_index("dev")
    my_y = me // X
    my_x = lax.rem(me, X)
    my_z = rd // 2
    my_c = lax.rem(rd, 2)

    def take(n, source, place):
        copy = pltpu.make_async_copy(source, place, copy_sem.at[n])
        copy.start()
        return copy

    own_a = take(0, win_in.at[:, pl.ds(0, HD)], w_a.at[me])
    own_b = take(1, win_in.at[:, pl.ds(HD, HD)], w_b.at[me])
    own_twi = take(2, twi_in, twi.at[rd])
    own_two = take(3, two_in, two.at[rd])
    own_out = take(4, wout_in, w_out.at[my_y, my_x])
    own_src = take(5, src_in, src)
    own_edges = take(6, edges_in, edges)

    def col(dx):
        return lax.rem(my_x + dx + X, X)

    def row(dy):
        return lax.rem(my_y + dy + Y, Y)

    def at(dy, dx):
        return row(dy) * X + col(dx)

    def zc(dz, dc=0):
        return lax.rem(my_z + dz + Z, Z) * 2 + lax.rem(my_c + dc, 2)

    barrier = pltpu.get_barrier_semaphore()

    def greet_dev(i, c):
        pl.semaphore_signal(
            barrier, inc=1, device_id={"dev": lax.rem(me + i, DV)}, device_id_type=MESH
        )
        return c

    def greet_rel(i, c):
        pl.semaphore_signal(
            barrier, inc=1, device_id={"rel": lax.rem(rd + i, R)}, device_id_type=MESH
        )
        return c

    lax.fori_loop(1, DV, greet_dev, 0)
    lax.fori_loop(1, R, greet_rel, 0)
    for copy in (own_a, own_b, own_twi, own_two, own_out, own_src, own_edges):
        copy.wait()
    pl.semaphore_wait(barrier, DV + R - 2)

    def remote(piece, place, sent, got, axis, to):
        pltpu.make_async_remote_copy(
            src_ref=piece,
            dst_ref=place,
            send_sem=sent,
            recv_sem=got,
            device_id={axis: to},
            device_id_type=MESH,
        ).start()

    def all_of(sem, view):
        pltpu.make_async_copy(view, view, sem).wait()

    half = (w_a, w_b)

    def push(h, block, to):
        piece = half[h].at[block]
        remote(piece, piece, ring_send_sem.at[h], ring_sem.at[h, block], "dev", to)

    def arrive(h, block):
        all_of(ring_sem.at[h, block], half[h].at[block])

    def begin_in():
        push(0, me, at(1, 0))
        push(0, me, at(-1, 0))
        push(0, me, at(0, 1))
        push(0, me, at(0, -1))
        push(1, me, at(1, 0))
        push(1, me, at(-1, 0))
        push(0, me, at(0, 2))
        push(1, me, at(0, 1))
        push(1, me, at(0, -1))

    def relay_x(dy):
        even = lax.rem(row(dy), 2) == 0
        arrive(1, at(dy, -1))
        arrive(1, at(dy, 1))
        push(
            1,
            jnp.where(even, at(dy, -1), at(dy, 1)),
            jnp.where(even, at(0, 1), at(0, -1)),
        )

    def first_half(s):
        def column(i, c):
            dx = jnp.where(i == 3, 2, jnp.where(i == 2, 3, i))
            if s == 0:
                arrive(0, at(0, dx))
                push(0, at(0, dx), at(1, 0))
                push(0, at(0, dx), at(-1, 0))
            elif s < HY:
                arrive(0, at(-s, dx))
                if s < HY - 1:
                    push(0, at(-s, dx), at(1, 0))
                arrive(0, at(s, dx))
                if s < HY - 1:
                    push(0, at(s, dx), at(-1, 0))
                else:
                    even = lax.rem(my_x + dx, 2) == 0
                    push(
                        0,
                        jnp.where(even, at(-s, dx), at(s, dx)),
                        jnp.where(even, at(1, 0), at(-1, 0)),
                    )
            else:
                arrive(0, at(HY, dx))
            return c

        lax.fori_loop(1 if s == 0 else 0, X, column, 0)

    def to_row(dy, far):
        push(1, at(dy, 0), at(0, 1))
        push(1, at(dy, 0), at(0, -1))
        if far:
            push(1, at(dy, 0), at(0, 2))

    def second_half(s):
        far = s >= HY - 1
        if 1 <= s < HY:
            for d in (-s, s):
                arrive(1, at(d, 0))
                if s < HY - 1:
                    push(1, at(d, 0), at(1 if d < 0 else -1, 0))
            if s == HY - 1:
                even = lax.rem(my_x, 2) == 0
                push(
                    1,
                    jnp.where(even, at(-s, 0), at(s, 0)),
                    jnp.where(even, at(1, 0), at(-1, 0)),
                )
            for d in (-s, s):
                to_row(d, far)
        elif s == HY:
            arrive(1, at(HY, 0))
            to_row(HY, far)
        if s == 1:
            relay_x(0)
        elif 2 <= s < HY:
            relay_x(-(s - 1))
            relay_x(s - 1)

    def second_rest():
        for d in (-(HY - 1), HY - 1, HY):
            arrive(1, at(d, 1))
            arrive(1, at(d, -1))
        if HY == 2:
            pass

        def rest(i, c):
            arrive(1, i * X + col(2))
            return c

        lax.fori_loop(0, Y, rest, 0)

    def out_push(y, to):
        piece = w_out.at[y, my_x]
        remote(piece, piece, wout_send_sem.at[0], y_sem.at[y], "dev", to)

    def out_arrive(y):
        all_of(y_sem.at[y], w_out.at[y, my_x])

    def out_y(s):
        if s == 0:
            out_push(my_y, at(1, 0))
            out_push(my_y, at(-1, 0))
        elif s < HY:
            out_arrive(row(-s))
            if s < HY - 1:
                out_push(row(-s), at(1, 0))
            out_arrive(row(s))
            if s < HY - 1:
                out_push(row(s), at(-1, 0))
            else:
                even = lax.rem(my_x, 2) == 0
                out_push(
                    jnp.where(even, row(-s), row(s)), jnp.where(even, at(1, 0), at(-1, 0))
                )
        else:
            out_arrive(row(HY))

    def out_part(c, x):
        return w_out.at[pl.ds(c * HY, HY), x]

    def out_x_begin():
        for side, c in ((0, 0), (1, 1), (0, 1), (1, 0)):
            piece = out_part(c, my_x)
            to = at(0, 1) if side == 0 else at(0, -1)
            remote(piece, piece, wout_send_sem.at[1], x_sem.at[side, c], "dev", to)

    def out_x_relay():
        for side in (0, 1):
            piece = out_part(side, col(-1) if side == 0 else col(1))
            all_of(x_sem.at[side, side], piece)
            to = at(0, 1) if side == 0 else at(0, -1)
            remote(piece, piece, wout_send_sem.at[1], far_sem.at[side], "dev", to)

    def out_x_rest():
        for side in (0, 1):
            all_of(x_sem.at[side, 1 - side], out_part(1 - side, col(-1) if side == 0 else col(1)))
        for side in (0, 1):
            all_of(far_sem.at[side], out_part(side, col(2)))

    tgt = (twi, two)

    def z_push(w, r, to):
        piece = tgt[w].at[r]
        remote(piece, piece, z_send_sem.at[w], z_sem.at[w, r], "rel", to)

    def z_arrive(w, r):
        all_of(z_sem.at[w, r], tgt[w].at[r])

    def z_step(s):
        for w in (0, 1):
            if s == 0:
                z_push(w, rd, zc(1))
                z_push(w, rd, zc(-1))
                z_push(w, rd, zc(0, 1))
            elif s < HZ:
                z_arrive(w, zc(-s))
                if s < HZ - 1 or w == 0:
                    z_push(w, zc(-s), zc(1))
                z_arrive(w, zc(s))
                if s < HZ - 1 or w == 1:
                    z_push(w, zc(s), zc(-1))
                z_push(w, zc(-s), zc(0, 1))
                z_push(w, zc(s), zc(0, 1))
            elif s == HZ:
                z_arrive(w, zc(HZ))
                z_push(w, zc(HZ), zc(0, 1))
            else:
                for d in range(Z):
                    z_arrive(w, zc(d, 1))

    def over_dev(n, piece, place, first=0, last=None):
        def send(i, c):
            to = lax.rem(me + i, DV)
            remote(piece(to), place, send_sem.at[n], recv_sem.at[n], "dev", to)
            return c

        lax.fori_loop(1, DV, send, 0)

    def folded(rows):
        return jnp.concatenate([rows[..., :HD], rows[..., HD:]], axis=-2).astype(BF)

    def count_tiles(first, number):
        lattice = lax.broadcasted_iota(jnp.int32, (TILE, TILE), 0).astype(F32).astype(BF)
        slots = lax.broadcasted_iota(jnp.int32, (1, TILE), 1)
        one = jnp.ones((TILE, TILE), BF)
        none = jnp.zeros((TILE, TILE), BF)

        def hot(spots):
            rows = jnp.broadcast_to(spots.astype(F32), (16, TILE)).astype(BF)
            return jnp.where(lattice == jnp.concatenate([rows] * (TILE // 16), axis=0), one, none)

        def some(i, c):
            for u in range(8):
                k = first + i * 8 + u
                codes = edges[pl.ds(k, 1), :]
                s_at = jnp.bitwise_and(codes, TILE - 1)
                t_at = jnp.where(slots < live[0, k], jnp.right_shift(codes, 7), -1)
                counts[k] = dot_nt(hot(s_at), hot(t_at)).astype(BF)
            return c

        lax.fori_loop(0, number // 8, some, 0)

    def slice_of(p):
        x = lax.rem(p, X)
        return (x // 2) * (DV // 2) + (p // X) * 2 + lax.rem(x, 2)

    mine = slice_of(me)
    my_rows = pl.ds(pl.multiple_of(mine * F, F), F)

    def rows_for(p):
        return pl.ds(pl.multiple_of(slice_of(p) * F, F), F)

    def first_projection(h):
        def some(j, c):
            cols = pl.ds(pl.multiple_of(j * W, W), W)
            value = dot_nn(src[...], half[h][:, :, cols].reshape(D, W))
            there = pl.ds(pl.multiple_of(h * HD + j * W, W), W)
            pre[:, there] = value
            turned = (value * jax.nn.sigmoid(value)).T.astype(BF)
            hid_t[0, there, :] = turned[:, :TILE]
            hid_t[1, there, :] = turned[:, TILE:]
            return c

        lax.fori_loop(0, HD // W, some, 0)

        def send(i, c):
            dy = i // 2
            to = row(dy) * X + 2 * h + lax.rem(my_x + lax.rem(i, 2), 2)

            @pl.when(to != me)
            def _():
                remote(
                    hid_t.at[:, rows_for(to), :],
                    hid_by_feature.at[pl.ds(2 * me, 2)],
                    send_sem.at[1],
                    recv_sem.at[1],
                    "dev",
                    to,
                )

            return c

        lax.fori_loop(0, DV // 2, send, 0)

    begin_in()
    z_step(0)
    for s in range(HY + 1):
        first_half(s)
        second_half(s)
        if s == HY - 1:
            z_step(1)
        if s != 1:
            out_y(max(s - 1, 0))
    first_projection(0)
    out_y(HY)
    second_rest()
    first_projection(1)
    hid_by_feature[pl.ds(2 * me, 2)] = hid_t[:, my_rows, :]
    out_x_begin()
    count_tiles(0, T)
    z_step(2)
    out_x_relay()
    all_of(recv_sem.at[1], hid_by_feature.at[pl.ds(0, 2 * (DV - 1))])

    def aggregate(i, c):
        for u in range(8):
            b = i * 8 + u
            total = jnp.zeros((F, TILE), F32)
            for q in range(TILE_ROW):
                k = b * TILE_ROW + q
                total = total + dot_nn(hid_by_feature[ids[0, k]], counts[k])
            agg_send[b] = total.astype(BF)
        return c

    lax.fori_loop(0, T // TILE_ROW // 8, aggregate, 0)
    over_dev(2, lambda to: agg_send.at[to], agg_recv.at[my_rows])
    agg_recv[my_rows, :] = agg_send[me]
    if HZ > 3:
        z_step(3)
    out_x_rest()
    all_of(recv_sem.at[2], agg_recv.at[pl.ds(0, D - F)])

    agg_hidden = agg_recv[...].astype(F32).T.astype(BF)
    for j in range(HD // W):
        low = dot_nn(agg_hidden, w_out[:, :, :, j * W : (j + 1) * W].reshape(D, W))
        high = dot_nn(agg_hidden, w_out[:, :, :, HD + j * W : HD + (j + 1) * W].reshape(D, W))
        both = jnp.concatenate([low.reshape(R, TR, W), high.reshape(R, TR, W)], axis=1)
        both = both.astype(BF).reshape(Z, 2, 2 * TR, W)
        part_send[0, :, :, j * W : (j + 1) * W] = both[:, 0]
        part_send[1, :, :, j * W : (j + 1) * W] = both[:, 1]
    remote(part_send.at[1 - my_c], part_pair, send_sem.at[0], recv_sem.at[0], "rel", zc(0, 1))
    if HZ > 2:
        z_step(HZ)

    def wide(rows):
        return (jnp.concatenate([rows, rows], axis=0) if TR < 16 else rows).astype(BF)

    all_of(recv_sem.at[0], part_pair)
    part_sum[...] = (part_send[my_c].astype(F32) + part_pair[...].astype(F32)).astype(BF)
    for d in range(1, Z):
        remote(
            part_sum.at[lax.rem(my_z + d, Z)],
            part_recv.at[my_z],
            send_sem.at[3],
            recv_sem.at[3],
            "rel",
            zc(d),
        )
    part_recv[my_z] = part_sum[my_z]
    z_step(HZ + 1)
    og_rows = wide(og[...].astype(F32))
    grad_hidden_t = [dot_nt(og_rows, two[r]) for r in range(R)]
    all_of(recv_sem.at[3], part_recv.at[pl.ds(0, Z - 1)])
    total = part_recv[0].astype(F32)
    for z in range(1, Z):
        total = total + part_recv[z].astype(F32)
    agg = jnp.concatenate([total[:TR], total[TR:]], axis=1)
    gain_row = gain[...]
    inverse_norm = lax.rsqrt(jnp.mean(agg * agg, axis=1, keepdims=True) + eps_norm)
    normed = wide(agg * inverse_norm * gain_row)
    target_pre = [dot_nn(normed, twi[r]) for r in range(R)]
    grad_normed = jnp.zeros((normed.shape[0], D), F32)
    for r in range(R):
        grad_pre_t = (grad_hidden_t[r] * silu_slope(target_pre[r])).astype(BF)
        grad_normed = grad_normed + dot_nt(grad_pre_t, twi[r])
    scaled = grad_normed[:TR] * gain_row
    mean_term = jnp.mean(agg * scaled, axis=1, keepdims=True)
    ga_send[...] = folded(
        inverse_norm * (scaled - agg * inverse_norm * inverse_norm * mean_term)
    )
    for dz in sorted(range(1, Z), key=lambda d: min(d, Z - d)):
        remote(ga_send, ga_recv.at[rd], send_sem.at[4], ga_sem.at[rd], "rel", zc(dz))
    remote(ga_send, ga_recv.at[rd], send_sem.at[4], ga_sem.at[rd], "rel", zc(0, 1))
    ga_recv[rd] = ga_send[...]
    update = jnp.zeros((normed.shape[0], D), F32)
    for r in range(R):
        target_hidden = (target_pre[r] * jax.nn.sigmoid(target_pre[r])).astype(BF)
        update = update + dot_nn(target_hidden, two[r])
    upd_out[...] = (tfeat[...].astype(F32) + update[:TR]).astype(BF)
    for dz in sorted(range(1, Z), key=lambda d: min(d, Z - d)):
        r = zc(dz)
        all_of(ga_sem.at[r], ga_recv.at[r])
        remote(ga_recv.at[r], ga_recv.at[r], send_sem.at[4], ga_sem.at[r], "rel", zc(0, 1))
    for dz in range(Z):
        r = zc(dz, 1)
        all_of(ga_sem.at[r], ga_recv.at[r])

    held = ga_recv[...].astype(F32)
    held = jnp.concatenate([held[:, :TR, :], held[:, TR:, :]], axis=2)
    grad_agg = held.reshape(R * TR, D).astype(BF)
    blocks = W // F
    for j in range(D // W):
        value = dot_nt(grad_agg, w_out[j * blocks // X : (j + 1) * blocks // X].reshape(W, D))
        gt_send[j * W : (j + 1) * W, :] = value.T.astype(BF)
    over_dev(5, lambda to: gt_send.at[rows_for(to)], gt_recv.at[me])
    gt_recv[me] = gt_send[my_rows, :]
    runs[T] = jnp.zeros((F, TILE), F32)
    all_of(recv_sem.at[5], gt_recv.at[pl.ds(0, DV - 1)])

    def spread(i, running):
        for u in range(32):
            j = i * 32 + u
            term = dot_nt(gt_recv[tab[1, j]], counts[tab[0, j]])
            running = running * tab[2, j].astype(F32) + term
            runs[j] = running
        return running

    lax.fori_loop(0, T // 32, spread, jnp.zeros((F, TILE), F32))

    def settle(i, c):
        for u in range(8):
            b = i * 8 + u
            gh_send[b] = runs[tab[3, b]].astype(BF)
        return c

    lax.fori_loop(0, 2 * DV // 8, settle, 0)
    over_dev(6, lambda to: gh_send.at[pl.ds(2 * to, 2)], gh_recv.at[:, my_rows, :])
    gh_recv[:, my_rows, :] = gh_send[pl.ds(2 * me, 2)]

    for h in range(2):
        all_of(ring_send_sem.at[h], half[h].at[pl.ds(0, DV - 1)])
        all_of(z_send_sem.at[h], tgt[h].at[pl.ds(0, R - 1)])
    all_of(wout_send_sem.at[0], w_out.at[pl.ds(0, Y - 1), 0])
    all_of(wout_send_sem.at[1], w_out.at[:, pl.ds(0, 3)])
    all_of(send_sem.at[0], part_pair)
    all_of(send_sem.at[1], hid_by_feature.at[pl.ds(0, 2 * (DV - 1))])
    all_of(send_sem.at[2], agg_recv.at[pl.ds(0, D - F)])
    all_of(send_sem.at[3], part_recv.at[pl.ds(0, Z - 1)])
    all_of(send_sem.at[4], ga_recv.at[pl.ds(0, R - 1)])
    all_of(send_sem.at[5], gt_recv.at[pl.ds(0, DV - 1)])

    all_of(recv_sem.at[6], gh_recv.at[:, pl.ds(0, D - F), :])

    def last_slope(j, c):
        cols = pl.ds(pl.multiple_of(j * W, W), W)
        turned = jnp.concatenate([gh_recv[0, cols, :], gh_recv[1, cols, :]], axis=1)
        value = turned.astype(F32).T * silu_slope(pre[:, cols])
        grad_pre[:, cols] = value.astype(BF)
        return c

    lax.fori_loop(0, D // W, last_slope, 0)

    def last_projection(j, c):
        cols = pl.ds(pl.multiple_of(j * W, W), W)
        these = pl.ds(j * blocks, blocks)
        value = dot_nt(grad_pre[:, :HD], w_a[these].reshape(W, HD))
        value = value + dot_nt(grad_pre[:, HD:], w_b[these].reshape(W, HD))
        grad_out[:, cols] = value.astype(BF)
        return c

    lax.fori_loop(0, D // W, last_projection, 0)
    all_of(send_sem.at[6], gh_recv.at[:, pl.ds(0, D - F), :])


def shards(
    src_feat,
    rel_w_in,
    rel_w_out,
    tile_source,
    tile_edges,
    tile_count,
    target_feat,
    norm_gain,
    tgt_w_in,
    tgt_w_out,
    out_grad,
):
    DV = lax.axis_size("dev")
    R = lax.axis_size("rel")
    own_rows = src_feat[0]
    rows, D = own_rows.shape
    F = D // DV
    T = tile_source.shape[1]
    TR = target_feat.shape[0]
    X, Y, Z = RING_X, DV // RING_X, R // 2
    HT = tgt_w_in.shape[1]
    tables = tile_tables(tile_source[0], rows * DV // TILE)

    vmem = pl.BlockSpec(memory_space=pltpu.VMEM)
    smem = pl.BlockSpec(memory_space=pltpu.SMEM)
    hbm = pl.BlockSpec(memory_space=pl.ANY)
    updated, grad_source = pl.pallas_call(
        functools.partial(whole_kernel, DV, R),
        out_shape=(
            jax.ShapeDtypeStruct((TR, D), BF),
            jax.ShapeDtypeStruct((rows, D), BF),
        ),
        in_specs=[smem] * 3 + [hbm] * 4 + [vmem] * 2 + [hbm] * 2 + [vmem],
        out_specs=(vmem, vmem),
        scratch_shapes=[
            pltpu.VMEM((rows, D), BF),
            pltpu.VMEM((T, TILE), jnp.int32),
            pltpu.VMEM((DV, F, D // 2), BF),
            pltpu.VMEM((DV, F, D // 2), BF),
            pltpu.VMEM((Y, X, F, D), BF),
            pltpu.VMEM((R, D, HT), BF),
            pltpu.VMEM((R, HT, D), BF),
            pltpu.VMEM((rows, D), F32),
            pltpu.VMEM((2, D, TILE), BF),
            pltpu.VMEM((2 * DV, F, TILE), BF),
            pltpu.VMEM((T, TILE, TILE), BF),
            pltpu.VMEM((DV, F, TILE), BF),
            pltpu.VMEM((D, TILE), BF),
            pltpu.VMEM((2, Z, 2 * TR, D // 2), BF),
            pltpu.VMEM((Z, 2 * TR, D // 2), BF),
            pltpu.VMEM((Z, 2 * TR, D // 2), BF),
            pltpu.VMEM((Z, 2 * TR, D // 2), BF),
            pltpu.VMEM((2 * TR, D // 2), BF),
            pltpu.VMEM((R, 2 * TR, D // 2), BF),
            pltpu.VMEM((D, TILE), BF),
            pltpu.VMEM((DV, F, TILE), BF),
            pltpu.VMEM((T + 1, F, TILE), F32),
            pltpu.VMEM((2 * DV, F, TILE), BF),
            pltpu.VMEM((2, D, TILE), BF),
            pltpu.VMEM((rows, D), BF),
            pltpu.SemaphoreType.DMA((7,)),
            pltpu.SemaphoreType.DMA((2, DV)),
            pltpu.SemaphoreType.DMA((2,)),
            pltpu.SemaphoreType.DMA((Y,)),
            pltpu.SemaphoreType.DMA((2, 2)),
            pltpu.SemaphoreType.DMA((2,)),
            pltpu.SemaphoreType.DMA((2,)),
            pltpu.SemaphoreType.DMA((2, R)),
            pltpu.SemaphoreType.DMA((2,)),
            pltpu.SemaphoreType.DMA((R,)),
            pltpu.SemaphoreType.DMA((7,)),
            pltpu.SemaphoreType.DMA((7,)),
        ],
        compiler_params=pltpu.CompilerParams(
            collective_id=0, has_side_effects=True, vmem_limit_bytes=60 * 1024 * 1024
        ),
        name="whole_layer",
    )(
        tile_source,
        tile_count,
        tables,
        own_rows,
        rel_w_in[0],
        rel_w_out[0],
        tile_edges[0],
        target_feat,
        norm_gain[None, :],
        tgt_w_in,
        tgt_w_out,
        out_grad,
    )
    return (updated, grad_source[None])


def solution(mesh):
    placed = (
        P("rel", "dev", None),
        P("rel", "dev", None),
        P("rel", "dev", None),
        P("rel", None),
        P("rel", None, None),
        P("rel", None),
        P(("dev", "rel"), None),
        P(),
        P(None, "rel"),
        P("rel", None),
        P(("dev", "rel"), None),
    )
    return jax.shard_map(
        shards,
        mesh=mesh,
        in_specs=placed,
        out_specs=(P(("dev", "rel"), None), P("rel", "dev", None)),
        check_vma=False,
    )
```

time: 153 us -> 123 us (0.80); the launches traced: 151 us -> 123 us
  Pallas kernels: 145 us -> 118 us
    pallas_call x1, Pallas kernels: 145 us -> 118 us  [shards(): pl.pallas_call(functools.partial(whole_kernel, DV, R), out_shape=(jax.Sha...]
where the time goes in v2:
time: 123 us
  Pallas kernels  118 us (96%)
  local copies, waits for them, and re-layouts  3.84 us (3%)
    pallas_call x1, Pallas kernels, shards(): pl.pallas_call(functools.partial(whole_kernel, DV, R), out_shape=(jax.Sha...  118 us
    unnamed x4, local copies, waits for them, and re-layouts  3.84 us

profile of v2, /device:TPU:1, one launch (start us, length us, event | category | flops | bytes accessed | tf_op | source)
XLA Modules:
  0.0 123.1 jit_solution(18379635731956822333)
XLA Ops:
  0.6 0.0 copy-start
  0.6 0.6 copy-done
  1.3 0.2 convert_reduce_fusion.1
  1.5 0.1 fusion.2
  1.6 0.1 select_reduce_fusion
  1.7 0.1 select_reduce_fusion.2
  1.9 0.6 pad_add_fusion.tab
  2.4 117.5 %whole_layer.1 = (bf16[8,1024]{1,0:T(8,128)(2,1)}, bf16[256,1024]{1,0:T(8,128)(2,1)}) custom-call(s32[1,128]{1,0:T(1,128)} %ids.1, s32[1,128]{1,0:T(1,128)} %live.1, s32[4,128]{1,0:T(4,128)} %pad_add_fusion.tab, bf16[256,1024]{1,0:T(8,128)(2,1)} %bitcast.14, bf16[32,1024]{1,0:T(8,128)(2,1)} %bitcast.16, bf16[32,1024]{1,0:T(8,128)(2,1)} %bitcast.17, ...), custom_call_target="tpu_custom_call" | custom-call | tf_op jit(solution)/shard_map/whole_layer/pallas_call | solution.py:634
  120.0 1.3 %copy.15 = bf16[8,1024]{1,0:T(8,128)(2,1)} copy(bf16[8,1024]{1,0:T(8,128)(2,1)} %get-tuple-element.13) | data formatting | bytes 32768
  121.3 1.9 %copy.16 = bf16[1,256,1024]{2,1,0:T(8,128)(2,1)} copy(bf16[1,256,1024]{2,1,0:T(8,128)(2,1)} %bitcast.15) | data formatting | bytes 1048576
  (4 shorter events, 0.0 us)
Async XLA Ops:
  0.6 0.7 copy-start

commit v3 on v2

--- a/solution.py
+++ b/solution.py
@@ -31,41 +31,30 @@
     return lax.dot_general(a, b, (((1,), (1,)), ((), ())), preferred_element_type=F32)
 
 
-def tile_tables(source_ids, source_blocks):
-    total = source_ids.shape[0]
-    spot = jnp.arange(total, dtype=jnp.int32)
-    earlier = (source_ids[None, :] < source_ids[:, None]) | (
-        (source_ids[None, :] == source_ids[:, None]) & (spot[None, :] < spot[:, None])
-    )
-    rank = jnp.sum(earlier.astype(jnp.int32), axis=1)
-    placed = rank[:, None] == spot[None, :]
-    order = jnp.sum(jnp.where(placed, spot[:, None], 0), axis=0)
-    here = jnp.sum(jnp.where(placed, source_ids[:, None], 0), axis=0)
-    before = jnp.sum(jnp.where(rank[:, None] + 1 == spot[None, :], source_ids[:, None] + 1, 0), axis=0) - 1
-    keep = (here == before).astype(jnp.int32)
-    named = source_ids[:, None] == spot[None, :]
-    upto = jnp.sum((source_ids[:, None] <= spot[None, :]).astype(jnp.int32), axis=0)
-    last = jnp.where(jnp.any(named, axis=0), upto - 1, total)
-    return jnp.stack([order, order // TILE_ROW, keep, last])
-
-
 def whole_kernel(
     DV,
     R,
-    ids,
-    live,
-    tab,
+    ids_in,
+    live_in,
     src_in,
     win_in,
     wout_in,
     edges_in,
+    tfeat_in,
+    gain_in,
+    twi_in,
+    two_in,
+    og_in,
+    upd_out,
+    grad_out,
+    ids,
+    live,
+    ids_v,
+    tab_v,
+    tab,
     tfeat,
     gain,
-    twi_in,
-    two_in,
     og,
-    upd_out,
-    grad_out,
     src,
     edges,
     w_a,
@@ -132,8 +121,16 @@
     own_twi = take(2, twi_in, twi.at[rd])
     own_two = take(3, two_in, two.at[rd])
     own_out = take(4, wout_in, w_out.at[my_y, my_x])
+    own_ids = take(7, ids_in, ids_v)
     own_src = take(5, src_in, src)
     own_edges = take(6, edges_in, edges)
+    own_small = [
+        take(8, ids_in, ids),
+        take(9, live_in, live),
+        take(10, tfeat_in, tfeat),
+        take(11, gain_in, gain),
+        take(12, og_in, og),
+    ]
 
     def col(dx):
         return lax.rem(my_x + dx + X, X)
@@ -149,23 +146,15 @@
 
     barrier = pltpu.get_barrier_semaphore()
 
-    def greet_dev(i, c):
-        pl.semaphore_signal(
-            barrier, inc=1, device_id={"dev": lax.rem(me + i, DV)}, device_id_type=MESH
-        )
-        return c
-
-    def greet_rel(i, c):
-        pl.semaphore_signal(
-            barrier, inc=1, device_id={"rel": lax.rem(rd + i, R)}, device_id_type=MESH
-        )
-        return c
-
-    lax.fori_loop(1, DV, greet_dev, 0)
-    lax.fori_loop(1, R, greet_rel, 0)
-    for copy in (own_a, own_b, own_twi, own_two, own_out, own_src, own_edges):
-        copy.wait()
-    pl.semaphore_wait(barrier, DV + R - 2)
+    near_dev = (at(1, 0), at(-1, 0), at(0, 1), at(0, -1), at(0, 2))
+    near_rel = (zc(1), zc(-1), zc(0, 1))
+    for to in near_dev:
+        pl.semaphore_signal(barrier, inc=1, device_id={"dev": to}, device_id_type=MESH)
+    for to in near_rel:
+        pl.semaphore_signal(barrier, inc=1, device_id={"rel": to}, device_id_type=MESH)
+    own_a.wait()
+    own_b.wait()
+    pl.semaphore_wait(barrier, len(near_dev) + len(near_rel))
 
     def remote(piece, place, sent, got, axis, to):
         pltpu.make_async_remote_copy(
@@ -307,27 +296,26 @@
         else:
             out_arrive(row(HY))
 
-    def out_part(c, x):
-        return w_out.at[pl.ds(c * HY, HY), x]
-
-    def out_x_begin():
-        for side, c in ((0, 0), (1, 1), (0, 1), (1, 0)):
-            piece = out_part(c, my_x)
-            to = at(0, 1) if side == 0 else at(0, -1)
-            remote(piece, piece, wout_send_sem.at[1], x_sem.at[side, c], "dev", to)
-
-    def out_x_relay():
-        for side in (0, 1):
-            piece = out_part(side, col(-1) if side == 0 else col(1))
-            all_of(x_sem.at[side, side], piece)
-            to = at(0, 1) if side == 0 else at(0, -1)
-            remote(piece, piece, wout_send_sem.at[1], far_sem.at[side], "dev", to)
-
-    def out_x_rest():
-        for side in (0, 1):
-            all_of(x_sem.at[side, 1 - side], out_part(1 - side, col(-1) if side == 0 else col(1)))
-        for side in (0, 1):
-            all_of(far_sem.at[side], out_part(side, col(2)))
+    def out_x(*rows):
+        for dy in rows:
+            piece = w_out.at[row(dy), my_x]
+            for side in (0, 1):
+                to = at(0, 1) if side == 0 else at(0, -1)
+                remote(piece, piece, wout_send_sem.at[1], x_sem.at[side, row(dy)], "dev", to)
+
+    def out_relay(*rows):
+        for dy in rows:
+            y = row(dy)
+            even = lax.rem(y, 2) == 0
+            all_of(x_sem.at[0, y], w_out.at[y, col(-1)])
+            all_of(x_sem.at[1, y], w_out.at[y, col(1)])
+            piece = w_out.at[y, jnp.where(even, col(-1), col(1))]
+            to = jnp.where(even, at(0, 1), at(0, -1))
+            remote(piece, piece, wout_send_sem.at[1], far_sem.at[y], "dev", to)
+
+    def out_far(*rows):
+        for dy in rows:
+            all_of(far_sem.at[row(dy)], w_out.at[row(dy), col(2)])
 
     tgt = (twi, two)
 
@@ -338,8 +326,8 @@
     def z_arrive(w, r):
         all_of(z_sem.at[w, r], tgt[w].at[r])
 
-    def z_step(s):
-        for w in (0, 1):
+    def z_step(s, weights=(0, 1)):
+        for w in weights:
             if s == 0:
                 z_push(w, rd, zc(1))
                 z_push(w, rd, zc(-1))
@@ -360,18 +348,19 @@
                 for d in range(Z):
                     z_arrive(w, zc(d, 1))
 
-    def over_dev(n, piece, place, first=0, last=None):
+    def over_dev(n, piece, place):
         def send(i, c):
-            to = lax.rem(me + i, DV)
+            m = (i + 1) // 2
+            to = lax.rem(me + DV // 2 + jnp.where(lax.rem(i, 2) == 1, m, DV - m), DV)
             remote(piece(to), place, send_sem.at[n], recv_sem.at[n], "dev", to)
             return c
 
-        lax.fori_loop(1, DV, send, 0)
+        lax.fori_loop(0, DV - 1, send, 0)
 
     def folded(rows):
         return jnp.concatenate([rows[..., :HD], rows[..., HD:]], axis=-2).astype(BF)
 
-    def count_tiles(first, number):
+    def count_tiles(first, number, turned=False):
         lattice = lax.broadcasted_iota(jnp.int32, (TILE, TILE), 0).astype(F32).astype(BF)
         slots = lax.broadcasted_iota(jnp.int32, (1, TILE), 1)
         one = jnp.ones((TILE, TILE), BF)
@@ -387,7 +376,9 @@
                 codes = edges[pl.ds(k, 1), :]
                 s_at = jnp.bitwise_and(codes, TILE - 1)
                 t_at = jnp.where(slots < live[0, k], jnp.right_shift(codes, 7), -1)
-                counts[k] = dot_nt(hot(s_at), hot(t_at)).astype(BF)
+                s_hot, t_hot = hot(s_at), hot(t_at)
+                pair = (t_hot, s_hot) if turned else (s_hot, t_hot)
+                counts[k] = dot_nt(*pair).astype(BF)
             return c
 
         lax.fori_loop(0, number // 8, some, 0)
@@ -434,24 +425,73 @@
 
         lax.fori_loop(0, DV // 2, send, 0)
 
+    def make_tables():
+        spread_ids = jnp.broadcast_to(ids_v[...], (T, T))
+        down = spread_ids.T
+        ii = lax.broadcasted_iota(jnp.int32, (T, T), 0)
+        jj = lax.broadcasted_iota(jnp.int32, (T, T), 1)
+
+        def over_tiles(mask, value):
+            return jnp.sum(jnp.where(mask, value, 0), axis=0, keepdims=True)
+
+        earlier = (down < spread_ids) | ((down == spread_ids) & (ii < jj))
+        rank = jnp.broadcast_to(over_tiles(earlier, 1), (T, T)).T
+        order = over_tiles(rank == jj, ii)
+        here = over_tiles(rank == jj, down)
+        before = over_tiles(rank + 1 == jj, down + 1) - 1
+        upto = over_tiles(down <= jj, 1)
+        named = over_tiles(down == jj, 1)
+        tab_v[0:1, :] = order
+        tab_v[1:2, :] = jnp.right_shift(order, 2)
+        tab_v[2:3, :] = jnp.where(here == before, 1, 0)
+        tab_v[3:4, :] = jnp.where(named > 0, upto - 1, T)
+
     begin_in()
+    own_twi.wait()
+    own_two.wait()
     z_step(0)
+    own_ids.wait()
+    make_tables()
+    own_tab = take(13, tab_v, tab)
+    own_out.wait()
+    soon = [d for n in range(HY - 1) for d in ((-n, n) if n else (0,))]
+    late = [-(HY - 1), HY - 1, HY]
     for s in range(HY + 1):
         first_half(s)
         second_half(s)
+        if s == 0:
+            out_x(0)
+        if s == HY - 2:
+            z_step(1, (0,))
+            out_y(0)
         if s == HY - 1:
-            z_step(1)
-        if s != 1:
-            out_y(max(s - 1, 0))
+            z_step(1, (1,))
+    out_y(1)
+    own_src.wait()
     first_projection(0)
-    out_y(HY)
+    out_x(*soon[1:3])
     second_rest()
     first_projection(1)
     hid_by_feature[pl.ds(2 * me, 2)] = hid_t[:, my_rows, :]
-    out_x_begin()
-    count_tiles(0, T)
-    z_step(2)
-    out_x_relay()
+    for s in range(2, HY - 1):
+        out_y(s)
+        out_x(-s, s)
+    out_relay(*soon[:3])
+    own_edges.wait()
+    for copy in own_small:
+        copy.wait()
+    own_tab.wait()
+    count_tiles(0, T // 2)
+    if HZ > 2:
+        z_step(2, (0,))
+    out_y(HY - 1)
+    out_x(-(HY - 1), HY - 1)
+    count_tiles(T // 2, T // 2)
+    if HZ > 2:
+        z_step(2, (1,))
+    out_y(HY)
+    out_x(HY)
+    out_relay(*soon[3:])
     all_of(recv_sem.at[1], hid_by_feature.at[pl.ds(0, 2 * (DV - 1))])
 
     def aggregate(i, c):
@@ -468,8 +508,13 @@
     over_dev(2, lambda to: agg_send.at[to], agg_recv.at[my_rows])
     agg_recv[my_rows, :] = agg_send[me]
     if HZ > 3:
-        z_step(3)
-    out_x_rest()
+        z_step(3, (0,))
+    out_relay(*late)
+    if HZ > 3:
+        z_step(3, (1,))
+    out_far(*soon)
+    out_far(*late)
+    z_step(HZ, (0,))
     all_of(recv_sem.at[2], agg_recv.at[pl.ds(0, D - F)])
 
     agg_hidden = agg_recv[...].astype(F32).T.astype(BF)
@@ -481,8 +526,6 @@
         part_send[0, :, :, j * W : (j + 1) * W] = both[:, 0]
         part_send[1, :, :, j * W : (j + 1) * W] = both[:, 1]
     remote(part_send.at[1 - my_c], part_pair, send_sem.at[0], recv_sem.at[0], "rel", zc(0, 1))
-    if HZ > 2:
-        z_step(HZ)
 
     def wide(rows):
         return (jnp.concatenate([rows, rows], axis=0) if TR < 16 else rows).astype(BF)
@@ -499,6 +542,7 @@
             zc(d),
         )
     part_recv[my_z] = part_sum[my_z]
+    z_step(HZ, (1,))
     z_step(HZ + 1)
     og_rows = wide(og[...].astype(F32))
     grad_hidden_t = [dot_nt(og_rows, two[r]) for r in range(R)]
@@ -547,12 +591,13 @@
     over_dev(5, lambda to: gt_send.at[rows_for(to)], gt_recv.at[me])
     gt_recv[me] = gt_send[my_rows, :]
     runs[T] = jnp.zeros((F, TILE), F32)
+    count_tiles(0, T, True)
     all_of(recv_sem.at[5], gt_recv.at[pl.ds(0, DV - 1)])
 
     def spread(i, running):
         for u in range(32):
             j = i * 32 + u
-            term = dot_nt(gt_recv[tab[1, j]], counts[tab[0, j]])
+            term = dot_nn(gt_recv[tab[1, j]], counts[tab[0, j]])
             running = running * tab[2, j].astype(F32) + term
             runs[j] = running
         return running
@@ -626,20 +671,26 @@
     TR = target_feat.shape[0]
     X, Y, Z = RING_X, DV // RING_X, R // 2
     HT = tgt_w_in.shape[1]
-    tables = tile_tables(tile_source[0], rows * DV // TILE)
 
     vmem = pl.BlockSpec(memory_space=pltpu.VMEM)
-    smem = pl.BlockSpec(memory_space=pltpu.SMEM)
-    hbm = pl.BlockSpec(memory_space=pl.ANY)
+    hbm = pl.BlockSpec(memory_space=pltpu.HBM)
     updated, grad_source = pl.pallas_call(
         functools.partial(whole_kernel, DV, R),
         out_shape=(
-            jax.ShapeDtypeStruct((TR, D), BF),
-            jax.ShapeDtypeStruct((rows, D), BF),
+            pltpu.VMEM((TR, D), BF),
+            pltpu.VMEM((rows, D), BF),
         ),
-        in_specs=[smem] * 3 + [hbm] * 4 + [vmem] * 2 + [hbm] * 2 + [vmem],
+        in_specs=[hbm] * 11,
         out_specs=(vmem, vmem),
         scratch_shapes=[
+            pltpu.SMEM((1, T), jnp.int32),
+            pltpu.SMEM((1, T), jnp.int32),
+            pltpu.VMEM((1, T), jnp.int32),
+            pltpu.VMEM((4, T), jnp.int32),
+            pltpu.SMEM((4, T), jnp.int32),
+            pltpu.VMEM((TR, D), BF),
+            pltpu.VMEM((1, D), F32),
+            pltpu.VMEM((TR, D), BF),
             pltpu.VMEM((rows, D), BF),
             pltpu.VMEM((T, TILE), jnp.int32),
             pltpu.VMEM((DV, F, D // 2), BF),
@@ -665,12 +716,12 @@
             pltpu.VMEM((2 * DV, F, TILE), BF),
             pltpu.VMEM((2, D, TILE), BF),
             pltpu.VMEM((rows, D), BF),
-            pltpu.SemaphoreType.DMA((7,)),
+            pltpu.SemaphoreType.DMA((14,)),
             pltpu.SemaphoreType.DMA((2, DV)),
             pltpu.SemaphoreType.DMA((2,)),
             pltpu.SemaphoreType.DMA((Y,)),
-            pltpu.SemaphoreType.DMA((2, 2)),
-            pltpu.SemaphoreType.DMA((2,)),
+            pltpu.SemaphoreType.DMA((2, Y)),
+            pltpu.SemaphoreType.DMA((Y,)),
             pltpu.SemaphoreType.DMA((2,)),
             pltpu.SemaphoreType.DMA((2, R)),
             pltpu.SemaphoreType.DMA((2,)),
@@ -685,7 +736,6 @@
     )(
         tile_source,
         tile_count,
-        tables,
         own_rows,
         rel_w_in[0],
         rel_w_out[0],

time: 123 us -> 111 us (0.902)
  Pallas kernels: 118 us -> 108 us
  local copies, waits for them, and re-layouts: 3.84 us -> 1.4 us
    pallas_call x1, Pallas kernels: 118 us -> 108 us  [shards(): pl.pallas_call(functools.partial(whole_kernel, DV, R), out_shape=(pltpu.V...]
    unnamed x4 -> x2, local copies, waits for them, and re-layouts: 3.84 us -> 1.4 us
where the time goes in v3:
time: 111 us; the launch traced here: 110 us
  Pallas kernels  108 us (97%)
  local copies, waits for them, and re-layouts  1.4 us (1%)
    pallas_call x1, Pallas kernels, shards(): pl.pallas_call(functools.partial(whole_kernel, DV, R), out_shape=(pltpu.V...  108 us

profile of v3, /device:TPU:1, one launch (start us, length us, event | category | flops | bytes accessed | tf_op | source)
XLA Modules:
  0.0 110.4 jit_solution(5933224186370213122)
XLA Ops:
  0.6 108.3 %whole_layer.1 = (bf16[8,1024]{1,0:T(8,128)(2,1)S(1)}, bf16[256,1024]{1,0:T(8,128)(2,1)S(1)}) custom-call(s32[1,128]{1,0:T(1,128)} %ids_in.1, s32[1,128]{1,0:T(1,128)} %live_in.1, bf16[256,1024]{1,0:T(8,128)(2,1)} %bitcast.7, bf16[32,1024]{1,0:T(8,128)(2,1)} %bitcast.8, bf16[32,1024]{1,0:T(8,128)(2,1)} %bitcast.9, s32[128,128]{1,0:T(8,128)} %bitcast.10, ...), custom_call_target="tpu_custom_call" | custom-call | tf_op jit(solution)/shard_map/whole_layer/pallas_call | solution.py:677
  109.0 0.6 copy.15
  109.6 0.8 copy.16

commit v4 on v3

--- a/solution.py
+++ b/solution.py
@@ -45,8 +45,8 @@
     twi_in,
     two_in,
     og_in,
-    upd_out,
-    grad_out,
+    upd_place,
+    grad_place,
     ids,
     live,
     ids_v,
@@ -80,6 +80,8 @@
     gh_send,
     gh_recv,
     grad_pre,
+    upd_out,
+    grad_out,
     copy_sem,
     ring_sem,
     ring_send_sem,
@@ -111,6 +113,26 @@
     my_z = rd // 2
     my_c = lax.rem(rd, 2)
 
+    def col(dx):
+        return lax.rem(my_x + dx + X, X)
+
+    def row(dy):
+        return lax.rem(my_y + dy + Y, Y)
+
+    def at(dy, dx):
+        return row(dy) * X + col(dx)
+
+    def zc(dz, dc=0):
+        return lax.rem(my_z + dz + Z, Z) * 2 + lax.rem(my_c + dc, 2)
+
+    barrier = pltpu.get_barrier_semaphore()
+
+    near_dev = (at(1, 0), at(-1, 0), at(0, 1), at(0, -1), at(0, 2))
+    near_rel = (zc(1), zc(-1), zc(0, 1))
+    for to in near_dev:
+        pl.semaphore_signal(barrier, inc=1, device_id={"dev": to}, device_id_type=MESH)
+    for to in near_rel:
+        pl.semaphore_signal(barrier, inc=1, device_id={"rel": to}, device_id_type=MESH)
     def take(n, source, place):
         copy = pltpu.make_async_copy(source, place, copy_sem.at[n])
         copy.start()
@@ -132,26 +154,6 @@
         take(12, og_in, og),
     ]
 
-    def col(dx):
-        return lax.rem(my_x + dx + X, X)
-
-    def row(dy):
-        return lax.rem(my_y + dy + Y, Y)
-
-    def at(dy, dx):
-        return row(dy) * X + col(dx)
-
-    def zc(dz, dc=0):
-        return lax.rem(my_z + dz + Z, Z) * 2 + lax.rem(my_c + dc, 2)
-
-    barrier = pltpu.get_barrier_semaphore()
-
-    near_dev = (at(1, 0), at(-1, 0), at(0, 1), at(0, -1), at(0, 2))
-    near_rel = (zc(1), zc(-1), zc(0, 1))
-    for to in near_dev:
-        pl.semaphore_signal(barrier, inc=1, device_id={"dev": to}, device_id_type=MESH)
-    for to in near_rel:
-        pl.semaphore_signal(barrier, inc=1, device_id={"rel": to}, device_id_type=MESH)
     own_a.wait()
     own_b.wait()
     pl.semaphore_wait(barrier, len(near_dev) + len(near_rel))
@@ -348,14 +350,22 @@
                 for d in range(Z):
                     z_arrive(w, zc(d, 1))
 
+    def wrap(i, n):
+        return i - jnp.where(i >= n, n, 0)
+
     def over_dev(n, piece, place):
-        def send(i, c):
-            m = (i + 1) // 2
-            to = lax.rem(me + DV // 2 + jnp.where(lax.rem(i, 2) == 1, m, DV - m), DV)
+        def send(to):
+            to = wrap(to, DV)
             remote(piece(to), place, send_sem.at[n], recv_sem.at[n], "dev", to)
+
+        send(me + DV // 2)
+
+        def pair(m, c):
+            send(me + DV // 2 - m)
+            send(me + DV // 2 + m)
             return c
 
-        lax.fori_loop(0, DV - 1, send, 0)
+        lax.fori_loop(1, DV // 2, pair, 0)
 
     def folded(rows):
         return jnp.concatenate([rows[..., :HD], rows[..., HD:]], axis=-2).astype(BF)
@@ -390,8 +400,30 @@
     mine = slice_of(me)
     my_rows = pl.ds(pl.multiple_of(mine * F, F), F)
 
-    def rows_for(p):
-        return pl.ds(pl.multiple_of(slice_of(p) * F, F), F)
+    def over_half(h, n, piece, place):
+        def send(y, near=False):
+            y = wrap(y, Y)
+            for bit in range(2):
+                to = y * X + 2 * h + bit
+
+                def one(to=to, bit=bit):
+                    part = pl.ds(pl.multiple_of((h * (DV // 2) + y * 2 + bit) * F, F), F)
+                    remote(piece(part), place, send_sem.at[n], recv_sem.at[n], "dev", to)
+
+                if near:
+                    pl.when(to != me)(one)
+                else:
+                    one()
+
+        send(my_y + HY)
+
+        def pair(m, c):
+            send(my_y + HY - m)
+            send(my_y + HY + m)
+            return c
+
+        lax.fori_loop(1, HY, pair, 0)
+        send(my_y, True)
 
     def first_projection(h):
         def some(j, c):
@@ -406,24 +438,9 @@
 
         lax.fori_loop(0, HD // W, some, 0)
 
-        def send(i, c):
-            dy = i // 2
-            to = row(dy) * X + 2 * h + lax.rem(my_x + lax.rem(i, 2), 2)
-
-            @pl.when(to != me)
-            def _():
-                remote(
-                    hid_t.at[:, rows_for(to), :],
-                    hid_by_feature.at[pl.ds(2 * me, 2)],
-                    send_sem.at[1],
-                    recv_sem.at[1],
-                    "dev",
-                    to,
-                )
-
-            return c
-
-        lax.fori_loop(0, DV // 2, send, 0)
+        over_half(
+            h, 1, lambda part: hid_t.at[:, part, :], hid_by_feature.at[pl.ds(2 * me, 2)]
+        )
 
     def make_tables():
         spread_ids = jnp.broadcast_to(ids_v[...], (T, T))
@@ -461,60 +478,70 @@
         second_half(s)
         if s == 0:
             out_x(0)
+        if s == HY - 3:
+            out_y(0)
         if s == HY - 2:
             z_step(1, (0,))
-            out_y(0)
         if s == HY - 1:
             z_step(1, (1,))
-    out_y(1)
+            out_y(1)
+            out_x(*soon[1:3])
+    for s in range(2, HY - 1):
+        out_y(s)
     own_src.wait()
     first_projection(0)
-    out_x(*soon[1:3])
-    second_rest()
-    first_projection(1)
-    hid_by_feature[pl.ds(2 * me, 2)] = hid_t[:, my_rows, :]
-    for s in range(2, HY - 1):
-        out_y(s)
-        out_x(-s, s)
-    out_relay(*soon[:3])
+    out_x(*soon[3:])
     own_edges.wait()
     for copy in own_small:
         copy.wait()
     own_tab.wait()
     count_tiles(0, T // 2)
+    second_rest()
+    out_y(HY - 1)
+    first_projection(1)
+    hid_by_feature[pl.ds(2 * me, 2)] = hid_t[:, my_rows, :]
+    out_x(-(HY - 1), HY - 1)
     if HZ > 2:
         z_step(2, (0,))
-    out_y(HY - 1)
-    out_x(-(HY - 1), HY - 1)
+    out_y(HY)
+    out_x(HY)
+    out_relay(*soon[:3])
     count_tiles(T // 2, T // 2)
     if HZ > 2:
         z_step(2, (1,))
-    out_y(HY)
-    out_x(HY)
+    all_of(recv_sem.at[1], hid_by_feature.at[pl.ds(0, 2 * (DV - 1))])
+
+    def sum_block(b):
+        total = jnp.zeros((F, TILE), F32)
+        for q in range(TILE_ROW):
+            k = b * TILE_ROW + q
+            total = total + dot_nn(hid_by_feature[ids[0, k]], counts[k])
+        agg_send[b] = total.astype(BF)
+
+    def send_block(b):
+        remote(agg_send.at[b], agg_recv.at[my_rows], send_sem.at[2], recv_sem.at[2], "dev", b)
+
+    def aggregate(i, c):
+        near = [i * 4 + u for u in range(4)]
+        pairs = [
+            (wrap(me + DV // 2 - m, DV), wrap(me + DV // 2 + 1 + m, DV)) for m in near
+        ]
+        for pair in pairs:
+            for b in pair:
+                sum_block(b)
+        for low, high in pairs:
+            send_block(low)
+            pl.when(high != me)(lambda high=high: send_block(high))
+        return c
+
+    lax.fori_loop(0, DV // 8, aggregate, 0)
+    agg_recv[my_rows, :] = agg_send[me]
     out_relay(*soon[3:])
-    all_of(recv_sem.at[1], hid_by_feature.at[pl.ds(0, 2 * (DV - 1))])
-
-    def aggregate(i, c):
-        for u in range(8):
-            b = i * 8 + u
-            total = jnp.zeros((F, TILE), F32)
-            for q in range(TILE_ROW):
-                k = b * TILE_ROW + q
-                total = total + dot_nn(hid_by_feature[ids[0, k]], counts[k])
-            agg_send[b] = total.astype(BF)
-        return c
-
-    lax.fori_loop(0, T // TILE_ROW // 8, aggregate, 0)
-    over_dev(2, lambda to: agg_send.at[to], agg_recv.at[my_rows])
-    agg_recv[my_rows, :] = agg_send[me]
-    if HZ > 3:
-        z_step(3, (0,))
     out_relay(*late)
     if HZ > 3:
-        z_step(3, (1,))
+        z_step(3)
     out_far(*soon)
     out_far(*late)
-    z_step(HZ, (0,))
     all_of(recv_sem.at[2], agg_recv.at[pl.ds(0, D - F)])
 
     agg_hidden = agg_recv[...].astype(F32).T.astype(BF)
@@ -532,7 +559,7 @@
 
     all_of(recv_sem.at[0], part_pair)
     part_sum[...] = (part_send[my_c].astype(F32) + part_pair[...].astype(F32)).astype(BF)
-    for d in range(1, Z):
+    for d in sorted(range(1, Z), key=lambda d: -min(d, Z - d)):
         remote(
             part_sum.at[lax.rem(my_z + d, Z)],
             part_recv.at[my_z],
@@ -542,7 +569,7 @@
             zc(d),
         )
     part_recv[my_z] = part_sum[my_z]
-    z_step(HZ, (1,))
+    z_step(HZ)
     z_step(HZ + 1)
     og_rows = wide(og[...].astype(F32))
     grad_hidden_t = [dot_nt(og_rows, two[r]) for r in range(R)]
@@ -564,7 +591,7 @@
     ga_send[...] = folded(
         inverse_norm * (scaled - agg * inverse_norm * inverse_norm * mean_term)
     )
-    for dz in sorted(range(1, Z), key=lambda d: min(d, Z - d)):
+    for dz in sorted(range(1, Z), key=lambda d: -min(d, Z - d)):
         remote(ga_send, ga_recv.at[rd], send_sem.at[4], ga_sem.at[rd], "rel", zc(dz))
     remote(ga_send, ga_recv.at[rd], send_sem.at[4], ga_sem.at[rd], "rel", zc(0, 1))
     ga_recv[rd] = ga_send[...]
@@ -573,6 +600,7 @@
         target_hidden = (target_pre[r] * jax.nn.sigmoid(target_pre[r])).astype(BF)
         update = update + dot_nn(target_hidden, two[r])
     upd_out[...] = (tfeat[...].astype(F32) + update[:TR]).astype(BF)
+    put_upd = take(14, upd_out, upd_place)
     for dz in sorted(range(1, Z), key=lambda d: min(d, Z - d)):
         r = zc(dz)
         all_of(ga_sem.at[r], ga_recv.at[r])
@@ -588,7 +616,9 @@
     for j in range(D // W):
         value = dot_nt(grad_agg, w_out[j * blocks // X : (j + 1) * blocks // X].reshape(W, D))
         gt_send[j * W : (j + 1) * W, :] = value.T.astype(BF)
-    over_dev(5, lambda to: gt_send.at[rows_for(to)], gt_recv.at[me])
+        if (j + 1) * W % HD == 0:
+            half_done = (j + 1) * W // HD - 1
+            over_half(half_done, 5, lambda part: gt_send.at[part], gt_recv.at[me])
     gt_recv[me] = gt_send[my_rows, :]
     runs[T] = jnp.zeros((F, TILE), F32)
     count_tiles(0, T, True)
@@ -611,7 +641,8 @@
         return c
 
     lax.fori_loop(0, 2 * DV // 8, settle, 0)
-    over_dev(6, lambda to: gh_send.at[pl.ds(2 * to, 2)], gh_recv.at[:, my_rows, :])
+    for h in range(2):
+        over_dev(6 + h, lambda to: gh_send.at[2 * to + h], gh_recv.at[h, my_rows, :])
     gh_recv[:, my_rows, :] = gh_send[pl.ds(2 * me, 2)]
 
     for h in range(2):
@@ -626,27 +657,47 @@
     all_of(send_sem.at[4], ga_recv.at[pl.ds(0, R - 1)])
     all_of(send_sem.at[5], gt_recv.at[pl.ds(0, DV - 1)])
 
-    all_of(recv_sem.at[6], gh_recv.at[:, pl.ds(0, D - F), :])
-
-    def last_slope(j, c):
+    def put_grad(h, j):
+        part = (pl.ds(h * TILE, TILE), pl.ds(pl.multiple_of(j * W, W), W))
+        return pltpu.make_async_copy(
+            grad_out.at[part], grad_place.at[part], copy_sem.at[15 + h * (D // W) + j]
+        )
+
+    def slopes(j, c):
         cols = pl.ds(pl.multiple_of(j * W, W), W)
-        turned = jnp.concatenate([gh_recv[0, cols, :], gh_recv[1, cols, :]], axis=1)
-        value = turned.astype(F32).T * silu_slope(pre[:, cols])
-        grad_pre[:, cols] = value.astype(BF)
+        pre[:, cols] = silu_slope(pre[:, cols])
         return c
 
-    lax.fori_loop(0, D // W, last_slope, 0)
-
-    def last_projection(j, c):
-        cols = pl.ds(pl.multiple_of(j * W, W), W)
-        these = pl.ds(j * blocks, blocks)
-        value = dot_nt(grad_pre[:, :HD], w_a[these].reshape(W, HD))
-        value = value + dot_nt(grad_pre[:, HD:], w_b[these].reshape(W, HD))
-        grad_out[:, cols] = value.astype(BF)
-        return c
-
-    lax.fori_loop(0, D // W, last_projection, 0)
-    all_of(send_sem.at[6], gh_recv.at[:, pl.ds(0, D - F), :])
+    lax.fori_loop(0, D // W, slopes, 0)
+
+    for h in range(2):
+        these_rows = slice(h * TILE, (h + 1) * TILE)
+        all_of(recv_sem.at[6 + h], gh_recv.at[h, pl.ds(0, D - F), :])
+
+        def last_slope(j, c):
+            cols = pl.ds(pl.multiple_of(j * W, W), W)
+            value = gh_recv[h, cols, :].astype(F32).T * pre[these_rows, cols]
+            grad_pre[these_rows, cols] = value.astype(BF)
+            return c
+
+        lax.fori_loop(0, D // W, last_slope, 0)
+
+        def last_projection(j, c):
+            cols = pl.ds(pl.multiple_of(j * W, W), W)
+            these = pl.ds(j * blocks, blocks)
+            value = dot_nt(grad_pre[these_rows, :HD], w_a[these].reshape(W, HD))
+            value = value + dot_nt(grad_pre[these_rows, HD:], w_b[these].reshape(W, HD))
+            grad_out[these_rows, cols] = value.astype(BF)
+            put_grad(h, j).start()
+            return c
+
+        lax.fori_loop(0, D // W, last_projection, 0)
+    put_upd.wait()
+    for h in range(2):
+        for j in range(D // W):
+            put_grad(h, j).wait()
+    for h in range(2):
+        all_of(send_sem.at[6 + h], gh_recv.at[h, pl.ds(0, D - F), :])
 
 
 def shards(
@@ -672,7 +723,8 @@
     X, Y, Z = RING_X, DV // RING_X, R // 2
     HT = tgt_w_in.shape[1]
 
-    vmem = pl.BlockSpec(memory_space=pltpu.VMEM)
+    place = pl.BlockSpec(memory_space=pl.ANY)
+    W = min(256, D // 2)
     hbm = pl.BlockSpec(memory_space=pltpu.HBM)
     updated, grad_source = pl.pallas_call(
         functools.partial(whole_kernel, DV, R),
@@ -681,7 +733,7 @@
             pltpu.VMEM((rows, D), BF),
         ),
         in_specs=[hbm] * 11,
-        out_specs=(vmem, vmem),
+        out_specs=(place, place),
         scratch_shapes=[
             pltpu.SMEM((1, T), jnp.int32),
             pltpu.SMEM((1, T), jnp.int32),
@@ -716,7 +768,9 @@
             pltpu.VMEM((2 * DV, F, TILE), BF),
             pltpu.VMEM((2, D, TILE), BF),
             pltpu.VMEM((rows, D), BF),
-            pltpu.SemaphoreType.DMA((14,)),
+            pltpu.VMEM((TR, D), BF),
+            pltpu.VMEM((rows, D), BF),
+            pltpu.SemaphoreType.DMA((15 + 2 * D // W,)),
             pltpu.SemaphoreType.DMA((2, DV)),
             pltpu.SemaphoreType.DMA((2,)),
             pltpu.SemaphoreType.DMA((Y,)),
@@ -726,8 +780,8 @@
             pltpu.SemaphoreType.DMA((2, R)),
             pltpu.SemaphoreType.DMA((2,)),
             pltpu.SemaphoreType.DMA((R,)),
-            pltpu.SemaphoreType.DMA((7,)),
-            pltpu.SemaphoreType.DMA((7,)),
+            pltpu.SemaphoreType.DMA((8,)),
+            pltpu.SemaphoreType.DMA((8,)),
         ],
         compiler_params=pltpu.CompilerParams(
             collective_id=0, has_side_effects=True, vmem_limit_bytes=60 * 1024 * 1024

time: 111 us -> 108 us (0.973); the launches traced: 110 us -> 109 us
    pallas_call x1, Pallas kernels: 108 us -> 107 us  [shards(): pl.pallas_call(functools.partial(whole_kernel, DV, R), out_shape=(pltpu.V...]
where the time goes in v4:
time: 108 us; the launch traced here: 109 us
  Pallas kernels  107 us (99%)
  local copies, waits for them, and re-layouts  1.4 us (1%)
    pallas_call x1, Pallas kernels, shards(): pl.pallas_call(functools.partial(whole_kernel, DV, R), out_shape=(pltpu.V...  107 us

profile of v4, /device:TPU:1, one launch (start us, length us, event | category | flops | bytes accessed | tf_op | source)
XLA Modules:
  0.0 108.6 jit_solution(12590946296482401768)
XLA Ops:
  0.6 106.5 %whole_layer.1 = (bf16[8,1024]{1,0:T(8,128)(2,1)S(1)}, bf16[256,1024]{1,0:T(8,128)(2,1)S(1)}) custom-call(s32[1,128]{1,0:T(1,128)} %ids_in.1, s32[1,128]{1,0:T(1,128)} %live_in.1, bf16[256,1024]{1,0:T(8,128)(2,1)} %bitcast.7, bf16[32,1024]{1,0:T(8,128)(2,1)} %bitcast.8, bf16[32,1024]{1,0:T(8,128)(2,1)} %bitcast.9, s32[128,128]{1,0:T(8,128)} %bitcast.10, ...), custom_call_target="tpu_custom_call" | custom-call | tf_op jit(solution)/shard_map/whole_layer/pallas_call | solution.py:729
  107.2 0.6 copy.15
  107.8 0.8 copy.16

commit v5 on v4

--- a/solution.py
+++ b/solution.py
@@ -90,8 +90,10 @@
     far_sem,
     wout_send_sem,
     z_sem,
+    z_pair_sem,
     z_send_sem,
     ga_sem,
+    ga_pair_sem,
     send_sem,
     recv_sem,
 ):
@@ -313,27 +315,30 @@
             all_of(x_sem.at[1, y], w_out.at[y, col(1)])
             piece = w_out.at[y, jnp.where(even, col(-1), col(1))]
             to = jnp.where(even, at(0, 1), at(0, -1))
-            remote(piece, piece, wout_send_sem.at[1], far_sem.at[y], "dev", to)
-
-    def out_far(*rows):
-        for dy in rows:
-            all_of(far_sem.at[row(dy)], w_out.at[row(dy), col(2)])
+            remote(piece, piece, wout_send_sem.at[1], far_sem.at[0], "dev", to)
+
+    def out_far():
+        all_of(far_sem.at[0], w_out.at[:, col(2)])
 
     tgt = (twi, two)
 
     def z_push(w, r, to):
         piece = tgt[w].at[r]
-        remote(piece, piece, z_send_sem.at[w], z_sem.at[w, r], "rel", to)
+        remote(piece, piece, z_send_sem.at[w], z_sem.at[w, lax.div(r, 2)], "rel", to)
+
+    def z_pair(w, r):
+        piece = tgt[w].at[r]
+        remote(piece, piece, z_send_sem.at[w], z_pair_sem.at[w], "rel", zc(0, 1))
 
     def z_arrive(w, r):
-        all_of(z_sem.at[w, r], tgt[w].at[r])
+        all_of(z_sem.at[w, lax.div(r, 2)], tgt[w].at[r])
 
     def z_step(s, weights=(0, 1)):
         for w in weights:
             if s == 0:
                 z_push(w, rd, zc(1))
                 z_push(w, rd, zc(-1))
-                z_push(w, rd, zc(0, 1))
+                z_pair(w, rd)
             elif s < HZ:
                 z_arrive(w, zc(-s))
                 if s < HZ - 1 or w == 0:
@@ -341,14 +346,13 @@
                 z_arrive(w, zc(s))
                 if s < HZ - 1 or w == 1:
                     z_push(w, zc(s), zc(-1))
-                z_push(w, zc(-s), zc(0, 1))
-                z_push(w, zc(s), zc(0, 1))
+                z_pair(w, zc(-s))
+                z_pair(w, zc(s))
             elif s == HZ:
                 z_arrive(w, zc(HZ))
-                z_push(w, zc(HZ), zc(0, 1))
+                z_pair(w, zc(HZ))
             else:
-                for d in range(Z):
-                    z_arrive(w, zc(d, 1))
+                all_of(z_pair_sem.at[w], tgt[w].at[pl.ds(0, Z)])
 
     def wrap(i, n):
         return i - jnp.where(i >= n, n, 0)
@@ -490,25 +494,25 @@
         out_y(s)
     own_src.wait()
     first_projection(0)
-    out_x(*soon[3:])
     own_edges.wait()
     for copy in own_small:
         copy.wait()
     own_tab.wait()
     count_tiles(0, T // 2)
+    out_y(HY - 1)
     second_rest()
-    out_y(HY - 1)
     first_projection(1)
     hid_by_feature[pl.ds(2 * me, 2)] = hid_t[:, my_rows, :]
+    out_x(*soon[3:])
     out_x(-(HY - 1), HY - 1)
     if HZ > 2:
         z_step(2, (0,))
     out_y(HY)
     out_x(HY)
     out_relay(*soon[:3])
-    count_tiles(T // 2, T // 2)
     if HZ > 2:
         z_step(2, (1,))
+    count_tiles(T // 2, T // 2)
     all_of(recv_sem.at[1], hid_by_feature.at[pl.ds(0, 2 * (DV - 1))])
 
     def sum_block(b):
@@ -540,8 +544,7 @@
     out_relay(*late)
     if HZ > 3:
         z_step(3)
-    out_far(*soon)
-    out_far(*late)
+    out_far()
     all_of(recv_sem.at[2], agg_recv.at[pl.ds(0, D - F)])
 
     agg_hidden = agg_recv[...].astype(F32).T.astype(BF)
@@ -592,8 +595,8 @@
         inverse_norm * (scaled - agg * inverse_norm * inverse_norm * mean_term)
     )
     for dz in sorted(range(1, Z), key=lambda d: -min(d, Z - d)):
-        remote(ga_send, ga_recv.at[rd], send_sem.at[4], ga_sem.at[rd], "rel", zc(dz))
-    remote(ga_send, ga_recv.at[rd], send_sem.at[4], ga_sem.at[rd], "rel", zc(0, 1))
+        remote(ga_send, ga_recv.at[rd], send_sem.at[4], ga_sem.at[my_z], "rel", zc(dz))
+    remote(ga_send, ga_recv.at[rd], send_sem.at[4], ga_pair_sem.at[0], "rel", zc(0, 1))
     ga_recv[rd] = ga_send[...]
     update = jnp.zeros((normed.shape[0], D), F32)
     for r in range(R):
@@ -603,11 +606,9 @@
     put_upd = take(14, upd_out, upd_place)
     for dz in sorted(range(1, Z), key=lambda d: min(d, Z - d)):
         r = zc(dz)
-        all_of(ga_sem.at[r], ga_recv.at[r])
-        remote(ga_recv.at[r], ga_recv.at[r], send_sem.at[4], ga_sem.at[r], "rel", zc(0, 1))
-    for dz in range(Z):
-        r = zc(dz, 1)
-        all_of(ga_sem.at[r], ga_recv.at[r])
+        all_of(ga_sem.at[lax.div(r, 2)], ga_recv.at[r])
+        remote(ga_recv.at[r], ga_recv.at[r], send_sem.at[4], ga_pair_sem.at[0], "rel", zc(0, 1))
+    all_of(ga_pair_sem.at[0], ga_recv.at[pl.ds(0, Z)])
 
     held = ga_recv[...].astype(F32)
     held = jnp.concatenate([held[:, :TR, :], held[:, TR:, :]], axis=2)
@@ -660,7 +661,7 @@
     def put_grad(h, j):
         part = (pl.ds(h * TILE, TILE), pl.ds(pl.multiple_of(j * W, W), W))
         return pltpu.make_async_copy(
-            grad_out.at[part], grad_place.at[part], copy_sem.at[15 + h * (D // W) + j]
+            grad_out.at[part], grad_place.at[part], copy_sem.at[15]
         )
 
     def slopes(j, c):
@@ -693,9 +694,7 @@
 
         lax.fori_loop(0, D // W, last_projection, 0)
     put_upd.wait()
-    for h in range(2):
-        for j in range(D // W):
-            put_grad(h, j).wait()
+    all_of(copy_sem.at[15], grad_out)
     for h in range(2):
         all_of(send_sem.at[6 + h], gh_recv.at[h, pl.ds(0, D - F), :])
 
@@ -724,7 +723,6 @@
     HT = tgt_w_in.shape[1]
 
     place = pl.BlockSpec(memory_space=pl.ANY)
-    W = min(256, D // 2)
     hbm = pl.BlockSpec(memory_space=pltpu.HBM)
     updated, grad_source = pl.pallas_call(
         functools.partial(whole_kernel, DV, R),
@@ -770,16 +768,18 @@
             pltpu.VMEM((rows, D), BF),
             pltpu.VMEM((TR, D), BF),
             pltpu.VMEM((rows, D), BF),
-            pltpu.SemaphoreType.DMA((15 + 2 * D // W,)),
+            pltpu.SemaphoreType.DMA((16,)),
             pltpu.SemaphoreType.DMA((2, DV)),
             pltpu.SemaphoreType.DMA((2,)),
             pltpu.SemaphoreType.DMA((Y,)),
             pltpu.SemaphoreType.DMA((2, Y)),
-            pltpu.SemaphoreType.DMA((Y,)),
+            pltpu.SemaphoreType.DMA((1,)),
             pltpu.SemaphoreType.DMA((2,)),
-            pltpu.SemaphoreType.DMA((2, R)),
+            pltpu.SemaphoreType.DMA((2, Z)),
             pltpu.SemaphoreType.DMA((2,)),
-            pltpu.SemaphoreType.DMA((R,)),
+            pltpu.SemaphoreType.DMA((2,)),
+            pltpu.SemaphoreType.DMA((Z,)),
+            pltpu.SemaphoreType.DMA((1,)),
             pltpu.SemaphoreType.DMA((8,)),
             pltpu.SemaphoreType.DMA((8,)),
         ],

time: 108 us -> 108 us (level)
  no operation moved by 1% of the time
where the time goes in v5:
time: 108 us
  Pallas kernels  106 us (98%)
  local copies, waits for them, and re-layouts  1.4 us (1%)
    pallas_call x1, Pallas kernels, shards(): pl.pallas_call(functools.partial(whole_kernel, DV, R), out_shape=(pltpu.V...  106 us

profile of v5, /device:TPU:1, one launch (start us, length us, event | category | flops | bytes accessed | tf_op | source)
XLA Modules:
  0.0 107.6 jit_solution(15469550716681353134)
XLA Ops:
  0.6 105.5 %whole_layer.1 = (bf16[8,1024]{1,0:T(8,128)(2,1)S(1)}, bf16[256,1024]{1,0:T(8,128)(2,1)S(1)}) custom-call(s32[1,128]{1,0:T(1,128)} %ids_in.1, s32[1,128]{1,0:T(1,128)} %live_in.1, bf16[256,1024]{1,0:T(8,128)(2,1)} %bitcast.7, bf16[32,1024]{1,0:T(8,128)(2,1)} %bitcast.8, bf16[32,1024]{1,0:T(8,128)(2,1)} %bitcast.9, s32[128,128]{1,0:T(8,128)} %bitcast.10, ...), custom_call_target="tpu_custom_call" | custom-call | tf_op jit(solution)/shard_map/whole_layer/pallas_call | solution.py:727
  106.2 0.6 copy.15
  106.8 0.8 copy.16

commit v6 on v5

--- a/solution.py
+++ b/solution.py
@@ -642,8 +642,7 @@
         return c
 
     lax.fori_loop(0, 2 * DV // 8, settle, 0)
-    for h in range(2):
-        over_dev(6 + h, lambda to: gh_send.at[2 * to + h], gh_recv.at[h, my_rows, :])
+    over_dev(6, lambda to: gh_send.at[pl.ds(2 * to, 2)], gh_recv.at[:, my_rows, :])
     gh_recv[:, my_rows, :] = gh_send[pl.ds(2 * me, 2)]
 
     for h in range(2):
@@ -671,9 +670,9 @@
 
     lax.fori_loop(0, D // W, slopes, 0)
 
+    all_of(recv_sem.at[6], gh_recv.at[:, pl.ds(0, D - F), :])
     for h in range(2):
         these_rows = slice(h * TILE, (h + 1) * TILE)
-        all_of(recv_sem.at[6 + h], gh_recv.at[h, pl.ds(0, D - F), :])
 
         def last_slope(j, c):
             cols = pl.ds(pl.multiple_of(j * W, W), W)
@@ -695,8 +694,7 @@
         lax.fori_loop(0, D // W, last_projection, 0)
     put_upd.wait()
     all_of(copy_sem.at[15], grad_out)
-    for h in range(2):
-        all_of(send_sem.at[6 + h], gh_recv.at[h, pl.ds(0, D - F), :])
+    all_of(send_sem.at[6], gh_recv.at[:, pl.ds(0, D - F), :])
 
 
 def shards(
@@ -780,8 +778,8 @@
             pltpu.SemaphoreType.DMA((2,)),
             pltpu.SemaphoreType.DMA((Z,)),
             pltpu.SemaphoreType.DMA((1,)),
-            pltpu.SemaphoreType.DMA((8,)),
-            pltpu.SemaphoreType.DMA((8,)),
+            pltpu.SemaphoreType.DMA((7,)),
+            pltpu.SemaphoreType.DMA((7,)),
         ],
         compiler_params=pltpu.CompilerParams(
             collective_id=0, has_side_effects=True, vmem_limit_bytes=60 * 1024 * 1024

time: 108 us -> 110 us (1.019)
  Pallas kernels: 106 us -> 108 us
    pallas_call x1, Pallas kernels: 106 us -> 108 us  [shards(): pl.pallas_call(functools.partial(whole_kernel, DV, R), out_shape=(pltpu.V...]
where the time goes in v6:
time: 110 us
  Pallas kernels  108 us (98%)
  local copies, waits for them, and re-layouts  1.4 us (1%)
    pallas_call x1, Pallas kernels, shards(): pl.pallas_call(functools.partial(whole_kernel, DV, R), out_shape=(pltpu.V...  108 us

profile of v6, /device:TPU:1, one launch (start us, length us, event | category | flops | bytes accessed | tf_op | source)
XLA Modules:
  0.0 109.6 jit_solution(4037888206508263907)
XLA Ops:
  0.6 107.6 %whole_layer.1 = (bf16[8,1024]{1,0:T(8,128)(2,1)S(1)}, bf16[256,1024]{1,0:T(8,128)(2,1)S(1)}) custom-call(s32[1,128]{1,0:T(1,128)} %ids_in.1, s32[1,128]{1,0:T(1,128)} %live_in.1, bf16[256,1024]{1,0:T(8,128)(2,1)} %bitcast.7, bf16[32,1024]{1,0:T(8,128)(2,1)} %bitcast.8, bf16[32,1024]{1,0:T(8,128)(2,1)} %bitcast.9, s32[128,128]{1,0:T(8,128)} %bitcast.10, ...), custom_call_target="tpu_custom_call" | custom-call | tf_op jit(solution)/shard_map/whole_layer/pallas_call | solution.py:725
  108.2 0.6 copy.15
  108.9 0.8 copy.16
